TPU v7x, 256 devices: a whole 4x4x8 slice. The times are simulated.
256 devices in a mesh: group: 8 (over y, z_hi), tp: 32 (over x, z_lo, core).
Axes of the slice: x: 4, y: 4, z: 8 (z_hi: 2, z_lo: 4; z = z_hi * 4 + z_lo), core: 2. Of those that a mesh axis runs over, the one named last changes fastest.
Arguments:
- queries: bfloat16 [8, 8, 2, 8192], P('group', None, None, 'tp'), may hold values from -24 to 24
- new_keys: bfloat16 [8, 8, 2, 1024], P('group', None, None, 'tp'), may hold values from -16 to 16
- new_values: bfloat16 [8, 8, 2, 1024], P('group', None, None, 'tp'), may hold values from -24 to 24
- key_pages: bfloat16 [8, 2048, 16, 1024], P('group', 'tp'), may hold values from -16 to 16
- value_pages: bfloat16 [8, 2048, 16, 1024], P('group', 'tp'), may hold values from -24 to 24
- page_owner: int32 [8, 2048], P('group', 'tp'), may hold values from 0 to 8, as said below
- page_fill: int32 [8, 2048], P('group', 'tp'), may hold values from 0 to 16, as said below
- target_slot: int32 [8, 8], P('group'), may hold values from 0 to 8, as said below
- out_weight: bfloat16 [8192, 8192], P(None, 'tp'), may hold values from -0.0625 to 0.0625
Outputs:
- projected: bfloat16 [8, 8, 2, 8192], P('group', None, None, 'tp')
Inputs may be any that keep to these rules, and one draw needn't show every extreme that they name: `page_owner`: the owning request slot, or 8 for a free page. Of each pair of groups g and g XOR (4) one is loaded (no free pages) and the other light; group 0 is light, and so is group 8 - 1 when 8 > 2. One device holds at most 16 pages of moving requests, and some device of every loaded group holds exactly 16. `page_fill`: 1 to 16 for a used page, 0 for a free one. `target_slot`: 8 for a request that stays. Every group has exactly one moving request; their slots in the partner group are distinct and own no pages there.
All inputs are finite; a program needn't handle non-finite values.
Results may differ from a plain program's by a relative error of at most 0.0065.
Values may be sent and summed in bfloat16 or wider, within the bound.
A program may use at most 64 MiB of HBM per device.

v0:
```python
import math

import jax
import jax.numpy as jnp
from jax import lax
from jax.sharding import PartitionSpec as P

HEADS = 64
KVH = 8
HD = 128
PAGE = 16
MOVE = 1


neg_big = -1e30


def side_by_side(arrays, axis, dim, along):
    ends, at = ([], 0)
    for a in arrays[:-1]:
        at += a.shape[along]
        ends.append(at)
    both = jnp.concatenate(arrays, axis=along)
    return tuple(jnp.split(lax.all_gather(both, axis, axis=dim, tiled=True), ends, axis=along))


def swapped(value, axis, distance):
    return lax.ppermute(value, axis, [(i, i ^ 1 << distance) for i in range(lax.axis_size(axis))])


def copy_for_each(value, axis):
    peers = lax.axis_size(axis)
    return lax.all_to_all(
        jnp.broadcast_to(value[None], (peers, *value.shape)), axis, 0, 0, tiled=True
    )


def taken_together(value, axis):
    return copy_for_each(value, axis).max(axis=0)


def split_up(value, dim, peers):
    before, after = (value.shape[:dim], value.shape[dim + 1 :])
    return jnp.moveaxis(value.reshape(*before, peers, -1, *after), dim, 0)


def summed_on_arrival(value, axis, dim):
    blocks = split_up(value, dim, lax.axis_size(axis))
    arrived = lax.all_to_all(blocks, axis, split_axis=0, concat_axis=0, tiled=True)
    return arrived.sum(axis=0)


def in_one_piece(arrays, axis, dim, along):
    columns = [a.reshape(*a.shape[:along], -1) for a in arrays]
    both = jnp.concatenate(columns, axis=along)
    out, at, finished = (summed_on_arrival(both, axis, dim), 0, [])
    for a, column in zip(arrays, columns):
        share = out[..., at : at + column.shape[along]]
        finished.append(share.reshape(*share.shape[:along], *a.shape[along:]))
        at += column.shape[along]
    return tuple(finished)


def laid_out(blocks, dim):
    blocks = jnp.moveaxis(blocks, 0, dim)
    shape = blocks.shape
    return blocks.reshape(*shape[:dim], shape[dim] * shape[dim + 1], *shape[dim + 2 :])


def collect(value, axis, dim):
    return laid_out(copy_for_each(value, axis), dim)


def merge_states(first, second):
    largest = jnp.maximum(first[0], second[0])
    scale_first = jnp.exp(first[0] - largest)
    scale_second = jnp.exp(second[0] - largest)
    return (
        largest,
        first[1] * scale_first + second[1] * scale_second,
        first[2] * scale_first[..., None] + second[2] * scale_second[..., None],
    )


def page_states(query_rows, key_block, value_block, owner_rows, fill_counts, row_count):
    page_count = key_block.shape[0]
    step_count = query_rows.shape[1]
    group_size = HEADS // KVH
    scale_factor = 1.0 / math.sqrt(HD)
    clipped = jnp.clip(owner_rows, 0, row_count - 1)
    query_page = jnp.take(query_rows, clipped, axis=0).reshape(
        page_count, step_count, KVH, group_size, HD
    )
    key_page = key_block.reshape(page_count, PAGE, KVH, HD)
    value_page = value_block.reshape(page_count, PAGE, KVH, HD)
    scores = (
        jnp.einsum("psgjd,ptgd->psgjt", query_page, key_page, preferred_element_type=jnp.float32)
        * scale_factor
    )
    live_token = (owner_rows < row_count)[:, None] & (
        lax.broadcasted_iota(jnp.int32, (page_count, PAGE), 1) < fill_counts[:, None]
    )
    token_mask = live_token[:, None, None, None, :]
    scores = jnp.where(token_mask, scores, neg_big)
    page_top = jnp.max(scores, axis=4).reshape(page_count, step_count * HEADS)
    member = owner_rows[None, :] == lax.broadcasted_iota(jnp.int32, (row_count, page_count), 0)
    row_top = jnp.max(jnp.where(member[:, :, None], page_top[None], neg_big), axis=1)
    top_page = jnp.take(row_top, clipped, axis=0).reshape(
        page_count, step_count, KVH, group_size, 1
    )
    weights = jnp.where(token_mask, jnp.exp(scores - top_page), 0.0).astype(jnp.bfloat16)
    weighted = jnp.einsum(
        "psgjt,ptgd->psgjd", weights, value_page, preferred_element_type=jnp.float32
    ).reshape(page_count, step_count * HEADS * HD)
    weight_sum = jnp.sum(weights.astype(jnp.float32), axis=4).reshape(
        page_count, step_count * HEADS
    )
    onehot = member.astype(jnp.float32)
    row_sum = jnp.dot(onehot, weight_sum)
    row_acc = jnp.dot(onehot, weighted)
    return (
        row_top.reshape(row_count, step_count, HEADS),
        row_sum.reshape(row_count, step_count, HEADS),
        row_acc.reshape(row_count, step_count, HEADS, HD),
    )


def new_token_states(query_heads, key_rows, value_rows, head_kv):
    row_count = key_rows.shape[0]
    step_count = key_rows.shape[1]
    scale_factor = 1.0 / math.sqrt(HD)
    key_heads = jnp.take(key_rows.reshape(row_count, step_count, KVH, HD), head_kv, axis=2)
    value_heads = jnp.take(
        value_rows.reshape(row_count, step_count, KVH, HD), head_kv, axis=2
    ).astype(jnp.float32)
    scores = (
        jnp.einsum("rshd,ruhd->rshu", query_heads, key_heads, preferred_element_type=jnp.float32)
        * scale_factor
    )
    causal = (
        lax.broadcasted_iota(jnp.int32, (step_count, step_count), 1)
        <= lax.broadcasted_iota(jnp.int32, (step_count, step_count), 0)
    )[None, :, None, :]
    scores = jnp.where(causal, scores, neg_big)
    largest = jnp.max(scores, axis=3)
    weights = jnp.where(causal, jnp.exp(scores - largest[..., None]), 0.0)
    return (largest, jnp.sum(weights, axis=3), jnp.einsum("rshu,ruhd->rshd", weights, value_heads))


def per_device(
    queries,
    new_keys,
    new_values,
    key_pages,
    value_pages,
    page_owner,
    page_fill,
    target_slot,
    out_weight,
):
    row_count = queries.shape[1]
    step_count = queries.shape[2]
    partner_bit = lax.axis_size("group").bit_length() - 2
    query_rows, key_rows, value_rows = (
        lax.all_gather(queries[0], "tp", axis=2, tiled=True),
        *side_by_side((new_keys[0], new_values[0]), "tp", 2, 0),
    )
    owners = page_owner[0]
    fill_counts = page_fill[0]
    slot_targets = target_slot[0]
    clipped = jnp.clip(owners, 0, row_count - 1)
    page_target = jnp.take(slot_targets, clipped)
    occupied = owners < row_count
    moving = occupied & (page_target < row_count)
    partner_targets = swapped(slot_targets, "group", partner_bit)
    slot_ids = lax.broadcasted_iota(jnp.int32, (row_count,), 0)
    mover_ids = lax.broadcasted_iota(jnp.int32, (MOVE, row_count), 0)
    their_moving = partner_targets < row_count
    their_rank = jnp.cumsum(their_moving.astype(jnp.int32)) - 1
    their_pick = their_moving[None, :] & (their_rank[None, :] == mover_ids)
    pick_rows = jnp.sum(their_pick.astype(jnp.int32) * partner_targets[None, :], axis=1)
    pick_valid = jnp.any(their_pick, axis=1)
    send_pick = pick_valid[:, None] & (pick_rows[:, None] == slot_ids[None, :])
    sent_queries = jnp.einsum(
        "mr,rsd->msd",
        send_pick.astype(jnp.bfloat16),
        query_rows,
        preferred_element_type=jnp.float32,
    ).astype(jnp.bfloat16)
    arrived_queries = swapped(sent_queries, "group", partner_bit)
    own_moving = slot_targets < row_count
    own_rank = jnp.cumsum(own_moving.astype(jnp.int32)) - 1
    page_rank = jnp.take(own_rank, clipped)
    local_rows = jnp.where(
        occupied, jnp.where(moving, row_count + page_rank, owners), row_count + MOVE
    )
    joined = page_states(
        jnp.concatenate([query_rows, arrived_queries], axis=0),
        key_pages[0],
        value_pages[0],
        local_rows,
        fill_counts,
        row_count + MOVE,
    )
    own_part = tuple((member_array[:row_count] for member_array in joined))
    theirs = tuple((member_array[row_count:] for member_array in joined))
    returned = swapped((theirs[0], theirs[1], theirs[2]), "group", partner_bit)
    placement_table = send_pick.astype(jnp.float32)
    placed_any = jnp.any(send_pick, axis=0)
    placed_max = jnp.where(
        placed_any[:, None, None], jnp.einsum("mr,msh->rsh", placement_table, returned[0]), neg_big
    )
    placed_sum = jnp.einsum("mr,msh->rsh", placement_table, returned[1])
    placed_acc = jnp.einsum("mr,mshd->rshd", placement_table, returned[2])
    states = merge_states(own_part, (placed_max, placed_sum, placed_acc))
    head_kv_all = lax.broadcasted_iota(jnp.int32, (HEADS,), 0) // (HEADS // KVH)
    query_heads = query_rows.reshape(row_count, step_count, HEADS, HD)
    largest = taken_together(states[0], "tp")
    shrink = jnp.exp(states[0] - largest)
    share_sum, share_acc = in_one_piece(
        (states[1] * shrink, states[2] * shrink[..., None]), "tp", 2, 3
    )
    share_heads = share_sum.shape[2]
    first_head = lax.axis_index("tp") * share_heads
    share_largest = lax.dynamic_slice_in_dim(largest, first_head, share_heads, 2)
    share_query = lax.dynamic_slice_in_dim(query_heads, first_head, share_heads, 2)
    share_kv = lax.dynamic_slice_in_dim(head_kv_all, first_head, share_heads, 0)
    new_terms = new_token_states(share_query, key_rows, value_rows, share_kv)
    finished = merge_states((share_largest, share_sum, share_acc), new_terms)
    share_attention = (finished[2] / finished[1][..., None]).astype(jnp.bfloat16)
    attention = collect(share_attention, "tp", 2).reshape(row_count * step_count, HEADS * HD)
    projected = jnp.dot(attention, out_weight, preferred_element_type=jnp.float32).astype(
        jnp.bfloat16
    )
    return projected.reshape(1, row_count, step_count, out_weight.shape[1])


def solution(mesh):
    placed = (
        P("group", None, None, "tp"),
        P("group", None, None, "tp"),
        P("group", None, None, "tp"),
        P("group", "tp", None, None),
        P("group", "tp", None, None),
        P("group", "tp"),
        P("group", "tp"),
        P("group", None),
        P(None, "tp"),
    )
    return jax.shard_map(
        per_device,
        mesh=mesh,
        in_specs=placed,
        out_specs=P("group", None, None, "tp"),
        check_vma=False,
    )
```

profile of v0, /device:TPU:1, one launch (start us, length us, event | category | flops | bytes accessed | tf_op | source)
XLA Modules:
  0.0 218.9 jit_solution(16080722643461589940)
XLA Ops:
  0.0 3.7 %collective-permute-start = (s32[8]{0:T(128)}, s32[8]{0:T(128)S(1)}, u32[]{:S(2)}, u32[]{:S(2)}) collective-permute-start(s32[8]{0:T(128)} %bitcast.157), channel_id=1, source_target_pairs={{0,128},{32,160},{64,192},{96,224},{128,0},{160,32},{192,64},{224,... | collective-permute-start | bytes 104 | tf_op jit(solution)/shard_map/ppermute | solution.py:28
  3.7 1.6 fusion.48
  5.4 0.7 fusion.37
  6.0 0.2 reduce-window.18
  6.2 0.7 fusion.49
  6.9 10.6 %broadcast_compare_fusion = (pred[64]{0:T(512)(128)(4,1)S(1)}, s32[64]{0:T(128)S(1)}) fusion(s32[]{:T(128)} %bitcast.19, s32[]{:T(128)} %bitcast.18, s32[]{:T(128)} %bitcast.17, s32[]{:T(128)} %bitcast.16, s32[]{:T(128)} %bitcast.15, s32[]{:T(128)} %bitcast.14, s32[]{:T(128)} %bitcast.13, s32[]{:T(128)} %bitcast.12, s32[]{:T(128)} %bitcast.9, s32[]{:T(128)} %bitcast.8, ...), kind=kLoop, calls=%fused_computation.116 | loop fusion | flops 2368 | bytes 640 | tf_op jit(solution)/shard_map/lt | solution.py:100
  17.5 46.4 %all-gather = bf16[1,8,2,8192]{3,2,1,0:T(2,128)(2,1)S(1)} all-gather(bf16[1,8,2,256]{3,2,1,0:T(2,128)(2,1)} %param.13), channel_id=2, replica_groups=mesh['group'=8,'tp'=32] {'tp'}, dimensions={3}, use_global_device_ids=true | all-gather | bytes 270336 | tf_op jit(solution)/shard_map/all_gather | solution.py:165
  63.9 2.2 %copy.230 = bf16[128,8,8,128]{3,2,1,0:T(8,128)(2,1)S(1)} copy(bf16[128,8,8,128]{3,1,2,0:T(8,128)(2,1)} %bitcast.143) | data formatting | bytes 4194304
  66.2 1.5 bitcast_bitcast_fusion.1
  67.7 0.9 copy-done.1
  68.5 0.6 copy.231
  69.2 1.5 bitcast_bitcast_fusion
  71.0 40.1 %all_gather.7 = bf16[16,2,1024]{0,1,2:T(2,128)(2,1)S(1)} all-gather(bf16[16,2,32]{0,1,2:T(2,128)(2,1)S(1)} %pad_maximum_fusion.1), channel_id=1, replica_groups=mesh['group'=8,'tp'=32] {'tp'}, dimensions={2}, use_global_device_ids=true | all-gather | bytes 67584 | tf_op jit(solution)/shard_map/all_gather | solution.py:24
  111.1 0.2 reduce-window.19
  111.3 0.6 fusion.43
  111.9 0.7 select_reduce_fusion.1
  112.7 1.3 compare_and_fusion.2
  114.0 0.4 fusion.17
  114.5 0.1 collective-permute-start.1
  114.6 1.3 fusion.38
  115.9 2.9 %collective-permute-done.1 = bf16[1,2,8192]{2,1,0:T(2,128)(2,1)S(1)} collective-permute-done((bf16[1,2,8192]{2,1,0:T(2,128)(2,1)S(1)}, bf16[1,2,8192]{2,1,0:T(2,128)(2,1)S(1)}, u32[]{:S(2)}, u32[]{:S(2)}) %collective-permute-start.1) | collective-permute-done | bytes 32800 | tf_op jit(solution)/shard_map/ppermute | solution.py:28
  118.8 0.4 pad_maximum_fusion
  119.2 6.1 %gather_fusion = bf16[64,2,8192]{2,1,0:T(2,128)(2,1)S(1)} fusion(bf16[9,2,8192]{2,1,0:T(2,128)(2,1)S(1)} %pad_maximum_fusion, s32[1024]{0:T(1024)S(1)} %pad_clamp_fusion.1), kind=kCustom, calls=%fused_computation.2 | custom fusion | bytes 4194560 | tf_op jit(solution)/shard_map/jit(_take)/gather | solution.py:91
  125.3 2.9 %gather.19 = bf16[64,2,8,8,128]{4,3,2,1,0:T(8,128)(2,1)} reshape(bf16[64,2,8192]{2,1,0:T(2,128)(2,1)S(1)} %gather_fusion) | data formatting | bytes 4194304 | tf_op jit(solution)/shard_map/jit(_take)/gather | solution.py:91
  128.1 5.8 %bitcast_reduce_fusion = (f32[64,2,8,8]{3,1,2,0:T(2,128)S(1)}, f32[64,8,2,8,16]{4,3,2,1,0:T(8,128)}) fusion(pred[64,16]{1,0:T(8,128)(4,1)S(1)} %fusion.20, bf16[64,16,8,128,1]{3,2,1,0,4:T(8,128)(2,1)} %bitcast_bitcast_fusion.1, bf16[64,2,8,8,128]{4,3,2,1,0:T(8,128)(2,1)} %gather.19, pred[64]{0:T(512)(128)(4,1)S(1)} %get-tuple-element.18), kind=kOutput, calls=%fused_computation.8 | convolution fusion | flops 34988032 | bytes 4752448 | tf_op jit(solution)/shard_map/psgjd,ptgd->psgjt/dot_general | solution.py:97
  134.0 0.3 copy.178
  134.3 0.2 select_reduce_fusion
  134.5 0.6 gather_fusion.1
  135.2 0.3 collective-permute-start.2
  135.6 0.4 copy.181
  136.1 5.7 %convert_reduce_fusion = bf16[64,2,8,8]{3,1,2,0:T(2,128)(2,1)} fusion(f32[64,2,8,8]{3,1,2,0:T(2,128)S(1)} %copy.181, f32[64,8,2,8,16]{4,3,2,1,0:T(8,128)} %get-tuple-element.41, pred[64,16]{1,0:T(8,128)(4,1)S(1)} %fusion.20), kind=kLoop, calls=%fused_computation.12 | loop fusion | flops 909312 | bytes 574464 | tf_op jit(solution)/shard_map/reduce_sum | solution.py:115
  141.8 2.0 convolution_bitcast_fusion
  143.8 0.5 copy.188
  144.3 1.2 fusion
  145.7 0.2 copy.182
  146.1 0.8 reshape.380
  146.9 5.1 %all-to-all-start = ((f32[32,1,1024]{2,1,0:T(1,128)}), f32[32,1,1024]{2,1,0:T(1,128)S(1)}, u32[]{:S(2)}, u32[]{:S(2)}) async-start(f32[32,1,1024]{2,1,0:T(1,128)} %reshape.380), calls=%async_computation | async-start | bytes 262144 | tf_op jit(solution)/shard_map/all_to_all | solution.py:33
  152.4 2.9 %collective-permute-start.3 = (f32[1,2,64]{2,1,0:T(2,128)S(1)}, f32[1,2,64]{2,1,0:T(2,128)S(1)}, u32[]{:S(2)}, u32[]{:S(2)}) collective-permute-start(f32[1,2,64]{2,1,0:T(2,128)S(1)} %slice.49), channel_id=1, source_target_pairs={{0,128},{32,160},{64,192},{96,224},{128,0},{160,32},{192,64},{224,... | collective-permute-start | bytes 1544 | tf_op jit(solution)/shard_map/ppermute | solution.py:28
  155.3 5.5 %all-to-all-done = f32[32,1,1024]{2,1,0:T(1,128)S(1)} async-done(((f32[32,1,1024]{2,1,0:T(1,128)}), f32[32,1,1024]{2,1,0:T(1,128)S(1)}, u32[]{:S(2)}, u32[]{:S(2)}) %all-to-all-start) | async-done | bytes 131104 | tf_op jit(solution)/shard_map/all_to_all | solution.py:33
  160.8 0.5 broadcast.372
  161.3 0.9 reduce.12
  162.9 0.8 copy.192
  163.7 0.5 add_multiply_fusion
  164.2 0.3 maximum_bitcast_fusion
  164.6 1.1 copy.193
  165.7 5.3 %all-to-all-start.1 = ((f32[32,8,2,2,129]{4,1,3,2,0:T(8,128)}), f32[32,8,2,2,129]{4,1,3,2,0:T(8,128)S(1)}, u32[]{:S(2)}, u32[]{:S(2)}) async-start(f32[32,8,2,2,129]{4,1,3,2,0:T(8,128)} %copy.193), calls=%async_computation.1 | async-start | bytes 2097152 | tf_op jit(solution)/shard_map/all_to_all | solution.py:49
  171.0 0.9 fusion.47
  171.9 0.3 copy.199
  172.3 0.3 copy.204
  172.7 0.6 gather_fusion.2
  173.3 0.6 gather_fusion.3
  173.9 0.2 fusion.50
  174.1 0.1 copy.201
  174.4 24.4 %all-to-all-done.1 = f32[32,8,2,2,129]{4,1,3,2,0:T(8,128)S(1)} async-done(((f32[32,8,2,2,129]{4,1,3,2,0:T(8,128)}), f32[32,8,2,2,129]{4,1,3,2,0:T(8,128)S(1)}, u32[]{:S(2)}, u32[]{:S(2)}) %all-to-all-start.1) | async-done | bytes 528416 | tf_op jit(solution)/shard_map/all_to_all | solution.py:49
  199.0 0.2 copy.227
  199.3 0.1 copy.202
  199.5 0.1 copy.211
  199.7 0.2 fusion.15
  199.9 0.1 broadcast_in_dim.166
  200.1 14.9 %all_to_all.15 = bf16[32,8,2,2,128]{4,3,2,1,0:T(2,128)(2,1)S(1)} all-to-all(bf16[32,8,2,2,128]{4,3,2,1,0:T(2,128)(2,1)S(1)} %broadcast_in_dim.166), channel_id=1, replica_groups=mesh['group'=8,'tp'=32] {'tp'}, dimensions={0} | all-to-all | bytes 524288 | tf_op jit(solution)/shard_map/all_to_all | solution.py:33
  215.0 0.2 copy.213
  215.2 0.2 reshape_reshape.3
  215.4 2.8 %convolution_convert_fusion = bf16[16,256]{1,0:T(8,128)(2,1)S(1)} fusion(bf16[16,8192]{1,0:T(8,128)(2,1)S(1)} %reshape_reshape.3, bf16[8192,256]{1,0:T(8,128)(2,1)} %param.21), kind=kOutput, calls=%fused_computation.30 | convolution fusion | flops 67112960 | bytes 4464640 | tf_op jit(solution)/shard_map/dot_general | solution.py:232
  218.3 0.6 reshape.270
  (64 shorter events, 2.8 us)
Async XLA Ops:
  0.0 111.1 %collective-permute-start = (s32[8]{0:T(128)}, s32[8]{0:T(128)S(1)}, u32[]{:S(2)}, u32[]{:S(2)}) collective-permute-start(s32[8]{0:T(128)} %bitcast.157), channel_id=1, source_target_pairs={{0,128},{32,160},{64,192},{96,224},{128,0},{160,32},{192,64},{224,... | collective-permute-start | bytes 104 | tf_op jit(solution)/shard_map/ppermute | solution.py:28
  66.2 2.4 %copy-start.1 = (bf16[1,64,16,1024]{3,2,1,0:T(8,128)(2,1)S(1)}, bf16[1,64,16,1024]{3,2,1,0:T(8,128)(2,1)}, u32[]{:S(2)}) copy-start(bf16[1,64,16,1024]{3,2,1,0:T(8,128)(2,1)} %param.17) | copy-start | bytes 6291460
  69.2 1.5 copy-start.4
  69.2 1.6 copy-start.5
  69.2 41.8 %copy-start.6 = (s32[1,64]{1,0:T(1,128)S(1)}, s32[1,64]{1,0:T(1,128)}, u32[]{:S(2)}) copy-start(s32[1,64]{1,0:T(1,128)} %param.19) | copy-start | bytes 772
  114.5 4.4 %collective-permute-start.1 = (bf16[1,2,8192]{2,1,0:T(2,128)(2,1)S(1)}, bf16[1,2,8192]{2,1,0:T(2,128)(2,1)S(1)}, u32[]{:S(2)}, u32[]{:S(2)}) collective-permute-start(bf16[1,2,8192]{2,1,0:T(2,128)(2,1)S(1)} %copy.277), channel_id=1, source_target_pairs={{0,128},{32,160},{64,192},{96,224},{128,0},{160,32},{192,64},{224,... | collective-permute-start | bytes 98312 | tf_op jit(solution)/shard_map/ppermute | solution.py:28
  133.9 7.9 %copy-start.2 = (bf16[64,16,8,128,1]{3,2,1,0,4:T(8,128)(2,1)S(1)}, bf16[64,16,8,128,1]{3,2,1,0,4:T(8,128)(2,1)}, u32[]{:S(2)}) copy-start(bf16[64,16,8,128,1]{3,2,1,0,4:T(8,128)(2,1)} %bitcast_bitcast_fusion) | copy-start | bytes 6291460
  135.2 10.8 %collective-permute-start.2 = (f32[1,2,64]{2,1,0:T(2,128)S(1)}, f32[1,2,64]{2,1,0:T(2,128)S(1)}, u32[]{:S(2)}, u32[]{:S(2)}) collective-permute-start(f32[1,2,64]{2,1,0:T(2,128)S(1)} %slice.47), channel_id=1, source_target_pairs={{0,128},{32,160},{64,192},{96,224},{128,0},{160,32},{192,64},{224,... | collective-permute-start | bytes 1544 | tf_op jit(solution)/shard_map/ppermute | solution.py:28
  136.1 5.7 %copy-start = (f32[64,8,2,8,16]{4,3,2,1,0:T(8,128)S(1)}, f32[64,8,2,8,16]{4,3,2,1,0:T(8,128)}, u32[]{:S(2)}) copy-start(f32[64,8,2,8,16]{4,3,2,1,0:T(8,128)} %get-tuple-element.41) | copy-start | bytes 1572868
  144.3 1.4 copy-start.3
  146.9 13.9 %all-to-all-start = ((f32[32,1,1024]{2,1,0:T(1,128)}), f32[32,1,1024]{2,1,0:T(1,128)S(1)}, u32[]{:S(2)}, u32[]{:S(2)}) async-start(f32[32,1,1024]{2,1,0:T(1,128)} %reshape.380), calls=%async_computation | async-start | bytes 262144 | tf_op jit(solution)/shard_map/all_to_all | solution.py:33
  152.4 10.1 %collective-permute-start.3 = (f32[1,2,64]{2,1,0:T(2,128)S(1)}, f32[1,2,64]{2,1,0:T(2,128)S(1)}, u32[]{:S(2)}, u32[]{:S(2)}) collective-permute-start(f32[1,2,64]{2,1,0:T(2,128)S(1)} %slice.49), channel_id=1, source_target_pairs={{0,128},{32,160},{64,192},{96,224},{128,0},{160,32},{192,64},{224,... | collective-permute-start | bytes 1544 | tf_op jit(solution)/shard_map/ppermute | solution.py:28
  155.2 8.5 %collective-permute-start.4 = (f32[1,2,64,128]{3,2,1,0:T(8,128)S(1)}, f32[1,2,64,128]{3,2,1,0:T(8,128)S(1)}, u32[]{:S(2)}, u32[]{:S(2)}) collective-permute-start(f32[1,2,64,128]{3,2,1,0:T(8,128)S(1)} %bitcast.156), channel_id=1, source_target_pairs={{0,128},{32,160},{64,192},{96,224},{128,0},{160,32},{192,64},{224,... | collective-permute-start | bytes 196616 | tf_op jit(solution)/shard_map/ppermute | solution.py:28
  165.7 33.2 %all-to-all-start.1 = ((f32[32,8,2,2,129]{4,1,3,2,0:T(8,128)}), f32[32,8,2,2,129]{4,1,3,2,0:T(8,128)S(1)}, u32[]{:S(2)}, u32[]{:S(2)}) async-start(f32[32,8,2,2,129]{4,1,3,2,0:T(8,128)} %copy.193), calls=%async_computation.1 | async-start | bytes 2097152 | tf_op jit(solution)/shard_map/all_to_all | solution.py:49
where the time goes:
time: 220 us; the launch traced here: 219 us
  blocking collectives  101 us (46%)
  waiting for transfers between devices  32.8 us (15%)
  local copies, waits for them, and re-layouts  29.4 us (13%)
  other arithmetic  24.5 us (11%)
  starting transfers between devices  17.6 us (8%)
  matrix products  12.8 us (6%)
    all_gather x1, blocking collectives, per_device(): lax.all_gather(queries[0], 'tp', axis=2, tiled=True)  46.4 us
    all_gather x1, blocking collectives, side_by_side(): lax.all_gather(both, axis, axis=dim, tiled=True)  40.1 us
    all_to_all x1, waiting for transfers between devices, summed_on_arrival(): lax.all_to_all(blocks, axis, split_axis=0, concat_axis=0, tiled=True)  24.4 us
    all_to_all x1, blocking collectives, copy_for_each(): lax.all_to_all(jnp.broadcast_to(value[None], (peers, *value.shape)), axis...  14.9 us
    lt x1, other arithmetic, page_states(): owner_rows < row_count  10.6 us
    gather x2, local copies, waits for them, and re-layouts, page_states(): jnp.take(query_rows, clipped, axis=0)  8.93 us
    ppermute x5, starting transfers between devices, swapped(): lax.ppermute(value, axis, [(i, i ^ 1 << distance) for i in range(lax.axis...  7.18 us
    dot_general x1, matrix products, page_states(): jnp.einsum('psgjd,ptgd->psgjt', query_page, key_page, preferred_element_t...  5.79 us
  transfers between devices with their start and end apart: 7, of which 3 were waited for; matrix products, arithmetic and copies ran while one was open for 17% of the time, Pallas kernels for 0%

commit v1 on v0

v1 whole, which is shorter than its diff:
```python
import functools
import math

import jax
import jax.numpy as jnp
from jax import lax
from jax.experimental import pallas as pl
from jax.experimental.pallas import tpu as pltpu
from jax.sharding import PartitionSpec as P

HD = 128
PAGE = 16
NZ = 4
NEG = -1e30
C2 = math.log2(math.e) / math.sqrt(HD)
MESH = pl.DeviceIdType.MESH
F32 = jnp.float32
BF16 = jnp.bfloat16


def iota(shape, dim):
    return lax.broadcasted_iota(jnp.int32, shape, dim)


def kernel(
    groups,
    nx,
    q_ref,
    nkv_ref,
    owner_ref,
    fill_ref,
    slot_ref,
    k_hbm,
    v_hbm,
    w_hbm,
    out_ref,
    k_ref,
    v_ref,
    w_ref,
    bias_ref,
    line_ref,
    part_ref,
    sib_ref,
    qall_ref,
    aout_ref,
    arecv_ref,
    stat_ref,
    sout_ref,
    srecv_ref,
    zacc_ref,
    zstat_ref,
    pout_ref,
    psout_ref,
    pacc_ref,
    pstat_ref,
    att_ref,
    load_sem,
    l_send,
    l_recv,
    p_send,
    p_recv,
    s_send,
    s_recv,
    q_send,
    q_recv,
    a_send,
    a_recv,
    t_send,
    t_recv,
    z_send,
    z_recv,
    y_send,
    y_recv,
    m_send,
    m_recv,
    n_send,
    n_recv,
    o_send,
    o_recv,
):
    np_ = nx * 2
    tokens = k_ref.shape[0]
    pages = owner_ref.shape[1]
    g = lax.axis_index("group")
    t = lax.axis_index("tp")
    x = lax.div(t, 8)
    z = lax.rem(lax.div(t, 2), NZ)
    c = lax.rem(t, 2)
    pp = x * 2 + c
    partner = lax.rem(g + groups // 2, groups)

    def on_plane(k):
        other = lax.rem(pp + k, np_)
        return other, (g, lax.div(other, 2) * 8 + z * 2 + lax.rem(other, 2))

    def on_line(group, k):
        other = lax.rem(z + k, NZ)
        return other, (group, x * 8 + other * 2 + c)

    def remote(src, dst, send, recv, device):
        return pltpu.make_async_remote_copy(
            src_ref=src,
            dst_ref=dst,
            send_sem=send,
            recv_sem=recv,
            device_id=device,
            device_id_type=MESH,
        )

    sent = []

    def send(*args):
        copy = remote(*args)
        copy.start()
        sent.append(copy)

    loads = [
        pltpu.make_async_copy(k_hbm, k_ref, load_sem.at[0]),
        pltpu.make_async_copy(v_hbm, v_ref, load_sem.at[1]),
        pltpu.make_async_copy(w_hbm, w_ref, load_sem.at[2]),
    ]
    for load in loads:
        load.start()

    barrier = pltpu.get_barrier_semaphore()
    greeted = 0
    for k in range(NZ):
        pl.semaphore_signal(barrier, inc=1, device_id=on_line(partner, k)[1], device_id_type=MESH)
        greeted += 1
    for k in range(1, NZ):
        pl.semaphore_signal(barrier, inc=1, device_id=on_line(g, k)[1], device_id_type=MESH)
        greeted += 1
    for k in range(1, np_):
        pl.semaphore_signal(barrier, inc=1, device_id=on_plane(k)[1], device_id_type=MESH)
        greeted += 1

    place = (iota((32, HD), 1) == iota((32, HD), 0) + 32 * lax.rem(t, 4)).astype(BF16)
    line_ref[z, 0:2] = q_ref[...]
    line_ref[z, 2] = jnp.dot(nkv_ref[0], place, preferred_element_type=F32).astype(BF16)
    line_ref[z, 3] = jnp.dot(nkv_ref[1], place, preferred_element_type=F32).astype(BF16)

    owned = jnp.where(
        jnp.broadcast_to(owner_ref[...], (8, pages)) == iota((8, pages), 0),
        jnp.broadcast_to(fill_ref[...], (8, pages)),
        0,
    )
    spread = (lax.div(iota((pages, tokens), 1), PAGE) == iota((pages, tokens), 0)).astype(BF16)
    held = jnp.dot(owned.astype(F32).astype(BF16), spread, preferred_element_type=F32)
    within = lax.rem(iota((8, tokens), 1), PAGE).astype(F32)
    bias_ref[...] = jnp.where(within < held, 0.0, NEG)

    slots = [slot_ref[0, r] for r in range(8)]
    row16 = lax.rem(iota((16, 32), 0), 8)
    target = jnp.full((16, 32), 8, jnp.int32)
    for r in range(8):
        target = jnp.where(row16 == r, slots[r], target)
    col = iota((16, 32), 1)
    step_row = lax.div(iota((16, 32), 0), 8)
    from_own = (target == 8) & (col == iota((16, 32), 0))
    from_other = (target < 8) & (col == 16 + step_row * 8 + target)
    pick = (from_own | from_other).astype(BF16)

    pl.semaphore_wait(barrier, greeted)

    for k in range(NZ):
        send(
            line_ref.at[z, 0:2], part_ref.at[z], p_send.at[k], p_recv.at[z], on_line(partner, k)[1]
        )
    for k in range(1, NZ):
        send(line_ref.at[z], line_ref.at[z], l_send.at[k], l_recv.at[z], on_line(g, k)[1])
    for k in range(1, NZ):
        other, device = on_line(g, k)
        remote(line_ref.at[z], line_ref.at[other], l_send.at[k], l_recv.at[other], device).wait_recv()
    for k in range(NZ):
        other, device = on_line(partner, k)
        remote(
            line_ref.at[z, 0:2], part_ref.at[other], p_send.at[k], p_recv.at[other], device
        ).wait_recv()

    for i in range(NZ):
        for e in range(2):
            both = jnp.concatenate([line_ref[i, e], part_ref[i, e]], axis=0)
            qall_ref[pp, i, e] = jnp.dot(pick, both, preferred_element_type=F32).astype(BF16)
    for k in range(1, np_):
        send(qall_ref.at[pp], qall_ref.at[pp], q_send.at[k], q_recv.at[pp], on_plane(k)[1])
    sibling = (g, x * 8 + z * 2 + (1 - c))
    send(line_ref.at[:, 2:4], sib_ref, s_send, s_recv, sibling)

    loads[0].wait()
    loads[1].wait()
    lane = iota((HD, HD), 1)
    stat_ref[...] = jnp.zeros((HD, HD), F32)
    for k in range(nx):
        xk = lax.rem(x + k, nx)
        for cc in range(2) if k else (1 - c,):
            other = xk * 2 + cc
            remote(
                qall_ref.at[pp], qall_ref.at[other], q_send.at[0], q_recv.at[other], sibling
            ).wait_recv()
        tops, sums = [], []
        for b in range(2):
            columns = pl.ds(pl.multiple_of((xk * 2 + b) * HD, HD), HD)
            query = jnp.concatenate(
                [qall_ref[xk * 2 + cc, 2 * b : 2 * b + 2].reshape(64, HD) for cc in range(2)], axis=0
            )
            score = lax.dot_general(
                query, k_ref[:, columns], (((1,), (1,)), ((), ())), preferred_element_type=F32
            )
            score = (score.reshape(16, 8, tokens) + bias_ref[...][None]).reshape(HD, tokens)
            top = jnp.max(score, axis=1, keepdims=True)
            weight = jnp.exp2((score - top) * C2)
            total = jnp.sum(weight, axis=1, keepdims=True)
            acc = jnp.dot(weight.astype(BF16), v_ref[:, columns], preferred_element_type=F32)
            acc = acc.astype(BF16)
            for cc in range(2):
                aout_ref[k, cc, b] = acc[cc * 64 : cc * 64 + 64]
            tops.append(top)
            sums.append(total)
        stat = stat_ref[...]
        for cc in range(2):
            part = slice(cc * 64, cc * 64 + 64)
            top = jnp.concatenate([tops[0][part], tops[1][part]], axis=0)
            total = jnp.concatenate([sums[0][part], sums[1][part]], axis=0)
            at = (k * 2 + cc) * 8
            stat = jnp.where(lane == at, top, jnp.where(lane == at + 1, total, stat))
        stat_ref[...] = stat
        for cc in range(2) if k else (1 - c,):
            device = (g, xk * 8 + z * 2 + cc)
            at = k * 2 + cc
            send(aout_ref.at[k, cc], arecv_ref.at[pp], a_send.at[at], a_recv.at[pp], device)
    turned = stat_ref[...].T
    for k in range(nx):
        for cc in range(2):
            at = k * 2 + cc
            sout_ref[at] = turned[at * 8 : at * 8 + 8]
    for k in range(nx):
        xk = lax.rem(x + k, nx)
        for cc in range(2) if k else (1 - c,):
            device = (g, xk * 8 + z * 2 + cc)
            at = k * 2 + cc
            send(sout_ref.at[at], srecv_ref.at[pp], t_send.at[at], t_recv.at[pp], device)
    arecv_ref[pp] = aout_ref[0, c]
    srecv_ref[pp] = sout_ref[c]

    remote(line_ref.at[:, 2:4], sib_ref, s_send, s_recv, sibling).wait_recv()
    tops, sums, news = [], [], []
    late = lax.rem(iota((8, 8, HD), 0), 2) == 1
    for b in range(2):
        new = [
            sum(
                line_ref[2 * b + i, 2 + kv].astype(F32) + sib_ref[2 * b + i, kv].astype(F32)
                for i in range(2)
            )
            for kv in range(2)
        ]
        query = line_ref[2 * b : 2 * b + 2, 0:2].astype(F32).reshape(8, 8, HD)
        first = jnp.sum(query * new[0][0:8][None], axis=2, keepdims=True)
        second = jnp.sum(query * new[0][8:16][None], axis=2, keepdims=True)
        first = jnp.broadcast_to(first, (8, 8, HD))
        second = jnp.where(late, jnp.broadcast_to(second, (8, 8, HD)), NEG)
        top = jnp.maximum(first, second)
        first = jnp.exp2((first - top) * C2)
        second = jnp.exp2((second - top) * C2)
        tops.append(top.reshape(64, HD))
        sums.append((first + second).reshape(64, HD))
        news.append((first * new[1][0:8][None] + second * new[1][8:16][None]).reshape(64, HD))
    new_acc = jnp.concatenate(news, axis=0)
    new_stat = jnp.where(
        lane == 0,
        jnp.concatenate(tops, axis=0),
        jnp.where(lane == 1, jnp.concatenate(sums, axis=0), 0.0),
    ).T
    new_top, new_sum = new_stat[0:1], new_stat[1:2]

    for k in range(1, np_):
        other, device = on_plane(k)
        remote(
            sout_ref.at[0], srecv_ref.at[other], t_send.at[0], t_recv.at[other], device
        ).wait_recv()
    tops = jnp.concatenate([srecv_ref[i, 0:1] for i in range(np_)], axis=0)
    sums = jnp.concatenate([srecv_ref[i, 1:2] for i in range(np_)], axis=0)
    top8 = jnp.max(tops, axis=0, keepdims=True)
    scale = jnp.exp2((tops - top8) * C2)
    sum8 = jnp.sum(scale * sums, axis=0, keepdims=True)
    scale = scale.T
    for k in range(1, np_):
        other, device = on_plane(k)
        remote(
            aout_ref.at[0, 0], arecv_ref.at[other], a_send.at[0], a_recv.at[other], device
        ).wait_recv()
    acc = jnp.zeros((HD, HD), F32)
    for i in range(np_):
        acc += scale[:, i : i + 1] * arecv_ref[i].reshape(HD, HD).astype(F32)
    acc = acc.astype(BF16)
    zacc_ref[z] = acc
    sub = iota((8, HD), 0)

    row = iota((16, HD), 1)
    at = lax.rem(row, 8)
    moves = jnp.zeros((16, HD), jnp.int32)
    for r in range(8):
        moves = jnp.where((at == r) & (slots[r] < 8), 1, moves)
    take = ((moves == 1) & (lax.div(row, 8) == iota((16, HD), 0))).astype(BF16)
    pout_ref[...] = jnp.dot(take, acc, preferred_element_type=F32).astype(BF16)
    moves = moves[0:8] == 1
    zstat_ref[z] = jnp.where(sub == 0, jnp.where(moves, NEG, top8), jnp.where(sub == 1, sum8, 0.0))
    goal = jnp.int32(8)
    for r in range(8):
        goal = jnp.where(slots[r] < 8, slots[r], goal)
    stat = jnp.where(sub == 0, top8, sum8)
    stat = jnp.where(moves, stat, NEG)
    within8 = lax.rem(iota((8, HD), 1), 8)
    for step in (1, 2, 4):
        low = lax.rem(lax.div(within8, step), 2) == 0
        swapped = jnp.where(low, pltpu.roll(stat, HD - step, 1), pltpu.roll(stat, step, 1))
        stat = jnp.maximum(stat, swapped)
    psout_ref[...] = jnp.where(within8 == goal, stat, jnp.where(sub == 0, NEG, 0.0))

    for k in range(NZ):
        device = on_line(partner, k)[1]
        send(pout_ref, pacc_ref.at[z], m_send.at[k], m_recv.at[z], device)
        send(psout_ref, pstat_ref.at[z], n_send.at[k], n_recv.at[z], device)
    for k in range(1, NZ):
        device = on_line(g, k)[1]
        send(zstat_ref.at[z], zstat_ref.at[z], y_send.at[k], y_recv.at[z], device)
        send(zacc_ref.at[z], zacc_ref.at[z], z_send.at[k], z_recv.at[z], device)
    for k in range(1, NZ):
        other, device = on_line(g, k)
        remote(
            zstat_ref.at[z], zstat_ref.at[other], y_send.at[k], y_recv.at[other], device
        ).wait_recv()
        remote(
            zacc_ref.at[z], zacc_ref.at[other], z_send.at[k], z_recv.at[other], device
        ).wait_recv()
    for k in range(NZ):
        other, device = on_line(partner, k)
        remote(pout_ref, pacc_ref.at[other], m_send.at[k], m_recv.at[other], device).wait_recv()
        remote(psout_ref, pstat_ref.at[other], n_send.at[k], n_recv.at[other], device).wait_recv()

    tops = jnp.concatenate(
        [zstat_ref[i, 0:1] for i in range(NZ)] + [pstat_ref[i, 0:1] for i in range(NZ)], axis=0
    )
    sums = jnp.concatenate(
        [zstat_ref[i, 1:2] for i in range(NZ)] + [pstat_ref[i, 1:2] for i in range(NZ)], axis=0
    )
    top = jnp.maximum(jnp.max(tops, axis=0, keepdims=True), new_top)
    scale = jnp.exp2((tops - top) * C2)
    new_scale = jnp.exp2((new_top - top) * C2)
    denominator = jnp.sum(scale * sums, axis=0, keepdims=True) + new_scale * new_sum
    scale = (scale / denominator).T
    new_scale = jnp.broadcast_to(new_scale / denominator, (8, HD)).T
    acc = new_scale[:, 0:1] * new_acc
    for i in range(NZ):
        acc += scale[:, i : i + 1] * zacc_ref[i].astype(F32)
        moved = jnp.broadcast_to(pacc_ref[i].astype(F32)[:, None, :], (16, 8, HD)).reshape(HD, HD)
        acc += scale[:, NZ + i : NZ + i + 1] * moved
    att_ref[pp] = acc.astype(BF16)
    for k in range(1, np_):
        send(att_ref.at[pp], att_ref.at[pp], o_send.at[k], o_recv.at[pp], on_plane(k)[1])

    loads[2].wait()
    result = jnp.zeros((16, out_ref.shape[1]), F32)
    for k in range(np_):
        other, device = on_plane(k)
        if k:
            remote(
                att_ref.at[pp], att_ref.at[other], o_send.at[k], o_recv.at[other], device
            ).wait_recv()
        block = att_ref[other]
        for i in range(NZ):
            at = lax.div(other, 2) * 8 + i * 2 + lax.rem(other, 2)
            rows = pl.ds(pl.multiple_of(at * 256, 256), 256)
            both = jnp.concatenate(
                [block[i * 32 : i * 32 + 16], block[i * 32 + 16 : i * 32 + 32]], axis=1
            )
            result += jnp.dot(both, w_ref[rows, :], preferred_element_type=F32)
    out_ref[...] = result.astype(BF16)
    for copy in sent:
        copy.wait_send()


def solution(mesh):
    groups, tp = mesh.shape["group"], mesh.shape["tp"]
    nx = tp // 8

    def per_device(queries, new_keys, new_values, key_pages, value_pages, owner, fill, slots, weight):
        tokens = key_pages.shape[1] * PAGE
        width = key_pages.shape[3]
        features, columns = weight.shape
        query = queries[0].reshape(8, 2, 2, HD).transpose(2, 1, 0, 3).reshape(2, 16, HD)
        new = jnp.stack([new_keys[0], new_values[0]]).transpose(0, 2, 1, 3).reshape(2, 16, 32)
        vmem = pl.BlockSpec(memory_space=pltpu.VMEM)
        smem = pl.BlockSpec(memory_space=pltpu.SMEM)
        hbm = pl.BlockSpec(memory_space=pl.ANY)
        np_ = 2 * nx
        dma = pltpu.SemaphoreType.DMA
        out = pl.pallas_call(
            functools.partial(kernel, groups, nx),
            out_shape=jax.ShapeDtypeStruct((16, columns), BF16),
            in_specs=[vmem, vmem, vmem, vmem, smem, hbm, hbm, hbm],
            out_specs=vmem,
            scratch_shapes=[
                pltpu.VMEM((tokens, width), BF16),
                pltpu.VMEM((tokens, width), BF16),
                pltpu.VMEM((features, columns), BF16),
                pltpu.VMEM((8, tokens), F32),
                pltpu.VMEM((NZ, 4, 16, HD), BF16),
                pltpu.VMEM((NZ, 2, 16, HD), BF16),
                pltpu.VMEM((NZ, 2, 16, HD), BF16),
                pltpu.VMEM((np_, NZ, 2, 16, HD), BF16),
                pltpu.VMEM((nx, 2, 2, 64, HD), BF16),
                pltpu.VMEM((np_, 2, 64, HD), BF16),
                pltpu.VMEM((HD, HD), F32),
                pltpu.VMEM((np_, 8, HD), F32),
                pltpu.VMEM((np_, 8, HD), F32),
                pltpu.VMEM((NZ, HD, HD), BF16),
                pltpu.VMEM((NZ, 8, HD), F32),
                pltpu.VMEM((16, HD), BF16),
                pltpu.VMEM((8, HD), F32),
                pltpu.VMEM((NZ, 16, HD), BF16),
                pltpu.VMEM((NZ, 8, HD), F32),
                pltpu.VMEM((np_, HD, HD), BF16),
                dma((3,)),
                dma((NZ,)),
                dma((NZ,)),
                dma((NZ,)),
                dma((NZ,)),
                dma,
                dma,
                dma((np_,)),
                dma((np_,)),
                dma((np_,)),
                dma((np_,)),
                dma((np_,)),
                dma((np_,)),
                dma((NZ,)),
                dma((NZ,)),
                dma((NZ,)),
                dma((NZ,)),
                dma((NZ,)),
                dma((NZ,)),
                dma((NZ,)),
                dma((NZ,)),
                dma((np_,)),
                dma((np_,)),
            ],
            compiler_params=pltpu.CompilerParams(
                collective_id=0, has_side_effects=True, vmem_limit_bytes=48 << 20
            ),
        )(
            query,
            new,
            owner,
            fill,
            slots,
            key_pages[0].reshape(tokens, width),
            value_pages[0].reshape(tokens, width),
            weight,
        )
        return out.reshape(2, 8, columns).transpose(1, 0, 2)[None]

    placed = (
        P("group", None, None, "tp"),
        P("group", None, None, "tp"),
        P("group", None, None, "tp"),
        P("group", "tp", None, None),
        P("group", "tp", None, None),
        P("group", "tp"),
        P("group", "tp"),
        P("group", None),
        P(None, "tp"),
    )
    return jax.shard_map(
        per_device,
        mesh=mesh,
        in_specs=placed,
        out_specs=P("group", None, None, "tp"),
        check_vma=False,
    )
```

time: 220 us -> 46.3 us (0.21)
  blocking collectives: 101 us -> 0 us
  Pallas kernels: 0 us -> 38.8 us
  waiting for transfers between devices: 32.8 us -> 0 us
  other arithmetic: 24.5 us -> 0.72 us
  local copies, waits for them, and re-layouts: 29.4 us -> 6.47 us
  starting transfers between devices: 17.6 us -> 0 us
  matrix products: 12.8 us -> 0 us
    all_gather x2 -> x0, blocking collectives: 86.5 us -> none  [the longest x1 46.4 us: per_device(): lax.all_gather(queries[0], 'tp', axis=2, tiled=True)]
    pallas_call x0 -> x1, Pallas kernels: none -> 38.8 us  [per_device(): pl.pallas_call(functools.partial(kernel, groups, nx), out_shape=jax.Shape...]
    all_to_all x2 -> x0, waiting for transfers between devices: 29.9 us -> none  [the longest x1 24.4 us: summed_on_arrival(): lax.all_to_all(blocks, axis, split_axis=0, concat_axis=0, tiled=True)]
    all_to_all x1 -> x0, blocking collectives: 14.9 us -> none  [copy_for_each(): lax.all_to_all(jnp.broadcast_to(value[None], (peers, *value.shape)), axis...]
    gather x8 -> x0, local copies, waits for them, and re-layouts: 13 us -> none  [the longest x2 8.93 us: page_states(): jnp.take(query_rows, clipped, axis=0)]
    dot_general x8 -> x0, matrix products: 12.8 us -> none  [the longest x1 5.79 us: page_states(): jnp.einsum('psgjd,ptgd->psgjt', query_page, key_page, preferred_element_t...]
    lt x1 -> x0, other arithmetic: 10.6 us -> none  [page_states(): owner_rows < row_count]
    all_to_all x2 -> x0, starting transfers between devices: 10.4 us -> none  [the longest x1 5.31 us: summed_on_arrival(): lax.all_to_all(blocks, axis, split_axis=0, concat_axis=0, tiled=True)]
  transfers between devices with their start and end apart: 7 -> 0, of which waited for: 3 -> 0; matrix products, arithmetic and copies ran while one was open for 17% -> 0% of each run, Pallas kernels for 0% -> 0%
where the time goes in v1:
time: 46.3 us; the launch traced here: 46 us
  Pallas kernels  38.8 us (84%)
  local copies, waits for them, and re-layouts  6.47 us (14%)
  other arithmetic  0.72 us (2%)
    pallas_call x1, Pallas kernels, per_device(): pl.pallas_call(functools.partial(kernel, groups, nx), out_shape=jax.Shape...  38.8 us
    unnamed x10, local copies, waits for them, and re-layouts  5.14 us

profile of v1, /device:TPU:1, one launch (start us, length us, event | category | flops | bytes accessed | tf_op | source)
XLA Modules:
  0.0 46.0 jit_solution(470826525605052144)
XLA Ops:
  0.0 0.7 %reshape_squeeze.9 = bf16[8,2,2,128]{3,2,1,0:T(2,128)(2,1)S(1)} reshape(bf16[1,8,2,256]{3,2,1,0:T(2,128)(2,1)} %param.9) | data formatting | bytes 16384 | tf_op jit(solution)/shard_map/reshape;squeeze | solution.py:390
  0.7 0.7 %maximum_bitcast_fusion = bf16[2,2,8,32]{3,1,2,0:T(2,128)(2,1)S(1)} fusion(bf16[1,8,2,32]{3,2,1,0:T(2,128)(2,1)} %param.11, bf16[1,8,2,32]{3,2,1,0:T(2,128)(2,1)} %param.10), kind=kLoop, calls=%fused_computation | loop fusion | flops 1024 | bytes 4096 | tf_op jit(solution)/shard_map/transpose | solution.py:391
  1.5 0.0 copy-start
  1.5 1.6 %copy-done = bf16[1,64,16,1024]{3,2,1,0:T(8,128)(2,1)S(1)} copy-done((bf16[1,64,16,1024]{3,2,1,0:T(8,128)(2,1)S(1)}, bf16[1,64,16,1024]{3,2,1,0:T(8,128)(2,1)}, u32[]{:S(2)}) %copy-start) | copy-done | bytes 2097176
  3.1 0.0 copy-start.1
  3.1 1.6 %copy-done.1 = bf16[1,64,16,1024]{3,2,1,0:T(8,128)(2,1)S(1)} copy-done((bf16[1,64,16,1024]{3,2,1,0:T(8,128)(2,1)S(1)}, bf16[1,64,16,1024]{3,2,1,0:T(8,128)(2,1)}, u32[]{:S(2)}) %copy-start.1) | copy-done | bytes 2097176
  4.6 0.0 copy-start.2
  4.6 0.7 %copy-done.2 = s32[1,64]{1,0:T(1,128)S(1)} copy-done((s32[1,64]{1,0:T(1,128)S(1)}, s32[1,64]{1,0:T(1,128)}, u32[]{:S(2)}) %copy-start.2) | copy-done | bytes 280
  5.3 0.0 copy-start.3
  5.3 0.7 %copy-done.3 = s32[1,64]{1,0:T(1,128)S(1)} copy-done((s32[1,64]{1,0:T(1,128)S(1)}, s32[1,64]{1,0:T(1,128)}, u32[]{:S(2)}) %copy-start.3) | copy-done | bytes 280
  6.0 0.0 copy-start.4
  6.0 0.7 %copy-done.4 = s32[1,8]{1,0:T(1,128)S(1)} copy-done((s32[1,8]{1,0:T(1,128)S(1)}, s32[1,8]{1,0:T(1,128)}, u32[]{:S(2)}) %copy-start.4) | copy-done | bytes 56
  6.6 38.8 %shard_map.91 = bf16[16,256]{1,0:T(8,128)(2,1)S(1)} custom-call(bf16[2,16,128]{2,1,0:T(8,128)(2,1)S(1)} %bitcast.20, bf16[2,16,32]{2,1,0:T(8,128)(2,1)S(1)} %bitcast.21, s32[1,64]{1,0:T(1,128)S(1)} %copy-done.2, s32[1,64]{1,0:T(1,128)S(1)} %copy-done.3, s32[1,8]{1,0:T(1,128)S(1)} %copy-done.4, bf16[1024,1024]{1,0:T(8,128)(2,1)S(1)} %bitcast.18, ...), custom_call_target="tpu_custom_call" | custom-call | tf_op jit(solution)/shard_map/pallas_call | solution.py:397
  45.4 0.6 %copy.16 = bf16[2,8,256]{2,0,1:T(2,128)(2,1)} copy(bf16[2,8,256]{2,1,0:T(8,128)(2,1)S(1)} %bitcast.22) | data formatting | bytes 16384 | tf_op jit(solution)/shard_map/reshape | solution.py:460
  (2 shorter events, 0.0 us)
Async XLA Ops:
  1.5 1.6 %copy-start = (bf16[1,64,16,1024]{3,2,1,0:T(8,128)(2,1)S(1)}, bf16[1,64,16,1024]{3,2,1,0:T(8,128)(2,1)}, u32[]{:S(2)}) copy-start(bf16[1,64,16,1024]{3,2,1,0:T(8,128)(2,1)} %param.12) | copy-start | bytes 6291460
  3.1 1.6 %copy-start.1 = (bf16[1,64,16,1024]{3,2,1,0:T(8,128)(2,1)S(1)}, bf16[1,64,16,1024]{3,2,1,0:T(8,128)(2,1)}, u32[]{:S(2)}) copy-start(bf16[1,64,16,1024]{3,2,1,0:T(8,128)(2,1)} %param.13) | copy-start | bytes 6291460
  4.6 0.7 %copy-start.2 = (s32[1,64]{1,0:T(1,128)S(1)}, s32[1,64]{1,0:T(1,128)}, u32[]{:S(2)}) copy-start(s32[1,64]{1,0:T(1,128)} %owner_ref.1) | copy-start | bytes 772
  5.3 0.7 %copy-start.3 = (s32[1,64]{1,0:T(1,128)S(1)}, s32[1,64]{1,0:T(1,128)}, u32[]{:S(2)}) copy-start(s32[1,64]{1,0:T(1,128)} %fill_ref.1) | copy-start | bytes 772
  6.0 0.7 %copy-start.4 = (s32[1,8]{1,0:T(1,128)S(1)}, s32[1,8]{1,0:T(1,128)}, u32[]{:S(2)}) copy-start(s32[1,8]{1,0:T(1,128)} %slot_ref.1) | copy-start | bytes 100

commit v2 on v1

--- a/solution.py
+++ b/solution.py
@@ -25,15 +25,22 @@
 def kernel(
     groups,
     nx,
+    q_hbm,
+    nk_hbm,
+    nv_hbm,
+    k_hbm,
+    v_hbm,
+    owner_hbm,
+    fill_hbm,
+    slot_hbm,
+    w_hbm,
+    out_ref,
     q_ref,
-    nkv_ref,
+    nk_ref,
+    nv_ref,
     owner_ref,
     fill_ref,
     slot_ref,
-    k_hbm,
-    v_hbm,
-    w_hbm,
-    out_ref,
     k_ref,
     v_ref,
     w_ref,
@@ -114,14 +121,19 @@
         copy.start()
         sent.append(copy)
 
-    loads = [
-        pltpu.make_async_copy(k_hbm, k_ref, load_sem.at[0]),
-        pltpu.make_async_copy(v_hbm, v_ref, load_sem.at[1]),
-        pltpu.make_async_copy(w_hbm, w_ref, load_sem.at[2]),
+    def fetch(src, dst, at):
+        copy = pltpu.make_async_copy(src, dst, load_sem.at[at])
+        copy.start()
+        return copy
+
+    small = [
+        fetch(q_hbm.at[0], q_ref, 3),
+        fetch(nk_hbm.at[0], nk_ref, 4),
+        fetch(nv_hbm.at[0], nv_ref, 5),
+        fetch(owner_hbm, owner_ref, 6),
+        fetch(fill_hbm, fill_ref, 7),
+        fetch(slot_hbm, slot_ref, 8),
     ]
-    for load in loads:
-        load.start()
-
     barrier = pltpu.get_barrier_semaphore()
     greeted = 0
     for k in range(NZ):
@@ -133,11 +145,25 @@
     for k in range(1, np_):
         pl.semaphore_signal(barrier, inc=1, device_id=on_plane(k)[1], device_id_type=MESH)
         greeted += 1
+    loads = [fetch(k_hbm, k_ref, 0), fetch(v_hbm, v_ref, 1), fetch(w_hbm, w_ref, 2)]
+    for copy in small:
+        copy.wait()
 
     place = (iota((32, HD), 1) == iota((32, HD), 0) + 32 * lax.rem(t, 4)).astype(BF16)
-    line_ref[z, 0:2] = q_ref[...]
-    line_ref[z, 2] = jnp.dot(nkv_ref[0], place, preferred_element_type=F32).astype(BF16)
-    line_ref[z, 3] = jnp.dot(nkv_ref[1], place, preferred_element_type=F32).astype(BF16)
+    order = (
+        iota((16, 16), 1)
+        == 2 * lax.rem(iota((16, 16), 0), 8) + lax.div(iota((16, 16), 0), 8)
+    ).astype(BF16)
+
+    def by_step(ref):
+        rows = ref[...].reshape(16, ref.shape[2])
+        return jnp.dot(order, rows, preferred_element_type=F32).astype(BF16)
+
+    query = by_step(q_ref)
+    line_ref[z, 0] = query[:, :HD]
+    line_ref[z, 1] = query[:, HD:]
+    line_ref[z, 2] = jnp.dot(by_step(nk_ref), place, preferred_element_type=F32).astype(BF16)
+    line_ref[z, 3] = jnp.dot(by_step(nv_ref), place, preferred_element_type=F32).astype(BF16)
 
     owned = jnp.where(
         jnp.broadcast_to(owner_ref[...], (8, pages)) == iota((8, pages), 0),
@@ -387,19 +413,22 @@
         tokens = key_pages.shape[1] * PAGE
         width = key_pages.shape[3]
         features, columns = weight.shape
-        query = queries[0].reshape(8, 2, 2, HD).transpose(2, 1, 0, 3).reshape(2, 16, HD)
-        new = jnp.stack([new_keys[0], new_values[0]]).transpose(0, 2, 1, 3).reshape(2, 16, 32)
         vmem = pl.BlockSpec(memory_space=pltpu.VMEM)
-        smem = pl.BlockSpec(memory_space=pltpu.SMEM)
         hbm = pl.BlockSpec(memory_space=pl.ANY)
         np_ = 2 * nx
         dma = pltpu.SemaphoreType.DMA
         out = pl.pallas_call(
             functools.partial(kernel, groups, nx),
             out_shape=jax.ShapeDtypeStruct((16, columns), BF16),
-            in_specs=[vmem, vmem, vmem, vmem, smem, hbm, hbm, hbm],
+            in_specs=[hbm] * 9,
             out_specs=vmem,
             scratch_shapes=[
+                pltpu.VMEM(queries.shape[1:], BF16),
+                pltpu.VMEM(new_keys.shape[1:], BF16),
+                pltpu.VMEM(new_values.shape[1:], BF16),
+                pltpu.VMEM(owner.shape, jnp.int32),
+                pltpu.VMEM(fill.shape, jnp.int32),
+                pltpu.SMEM(slots.shape, jnp.int32),
                 pltpu.VMEM((tokens, width), BF16),
                 pltpu.VMEM((tokens, width), BF16),
                 pltpu.VMEM((features, columns), BF16),
@@ -420,7 +449,7 @@
                 pltpu.VMEM((NZ, 16, HD), BF16),
                 pltpu.VMEM((NZ, 8, HD), F32),
                 pltpu.VMEM((np_, HD, HD), BF16),
-                dma((3,)),
+                dma((9,)),
                 dma((NZ,)),
                 dma((NZ,)),
                 dma((NZ,)),
@@ -445,16 +474,17 @@
                 dma((np_,)),
             ],
             compiler_params=pltpu.CompilerParams(
-                collective_id=0, has_side_effects=True, vmem_limit_bytes=48 << 20
+                collective_id=0, has_side_effects=True, vmem_limit_bytes=62 << 20
             ),
         )(
-            query,
-            new,
+            queries,
+            new_keys,
+            new_values,
+            key_pages[0].reshape(tokens, width),
+            value_pages[0].reshape(tokens, width),
             owner,
             fill,
             slots,
-            key_pages[0].reshape(tokens, width),
-            value_pages[0].reshape(tokens, width),
             weight,
         )
         return out.reshape(2, 8, columns).transpose(1, 0, 2)[None]

time: 46.3 us -> 40.1 us (0.87)
  local copies, waits for them, and re-layouts: 6.47 us -> 1.3 us
  other arithmetic: 0.72 us -> 0 us
    unnamed x10 -> x0, local copies, waits for them, and re-layouts: 5.14 us -> none
    transpose x1 -> x0, other arithmetic: 0.72 us -> none  [per_device(): jnp.stack([new_keys[0], new_values[0]]).transpose(0, 2, 1, 3)]
    another operation x2 -> x0, local copies, waits for them, and re-layouts: 0.72 us -> none  [per_device(): queries[0].reshape(8, 2, 2, HD).transpose(2, 1, 0, 3).reshape(2, 16, HD)]
    reshape x1, local copies, waits for them, and re-layouts: 0.61 us -> 1.3 us  [per_device(): return out.reshape(2, 8, columns).transpose(1, 0, 2)[None]]
where the time goes in v2:
time: 40.1 us; the launch traced here: 39.9 us
  Pallas kernels  38.6 us (96%)
  local copies, waits for them, and re-layouts  1.3 us (3%)
    pallas_call x1, Pallas kernels, per_device(): pl.pallas_call(functools.partial(kernel, groups, nx), out_shape=jax.Shape...  38.6 us
    reshape x1, local copies, waits for them, and re-layouts, per_device(): return out.reshape(2, 8, columns).transpose(1, 0, 2)[None]  1.3 us

profile of v2, /device:TPU:1, one launch (start us, length us, event | category | flops | bytes accessed | tf_op | source)
XLA Modules:
  0.0 39.9 jit_solution(12883749145297564615)
XLA Ops:
  0.0 38.6 %shard_map.91 = bf16[16,256]{1,0:T(8,128)(2,1)} custom-call(bf16[1,8,2,256]{3,2,1,0:T(2,128)(2,1)} %q_hbm.1, bf16[1,8,2,32]{3,2,1,0:T(2,128)(2,1)} %nk_hbm.1, bf16[1,8,2,32]{3,2,1,0:T(2,128)(2,1)} %nv_hbm.1, bf16[1024,1024]{1,0:T(8,128)(2,1)} %bitcast.8, bf16[1024,1024]{1,0:T(8,128)(2,1)} %bitcast.9, s32[1,64]{1,0:T(1,128)} %owner_hbm.1, s32[1,64]{1,0:T(1,128)} %fill_hbm.1, ...), custom_call_target="tpu_custom_call" | custom-call | tf_op jit(solution)/shard_map/pallas_call | solution.py:420
  38.6 1.3 %copy.12 = bf16[2,8,256]{2,0,1:T(2,128)(2,1)} copy(bf16[2,8,256]{2,1,0:T(8,128)(2,1)} %bitcast.10) | data formatting | bytes 16384 | tf_op jit(solution)/shard_map/reshape | solution.py:490

commit v3 on v2

v3 whole, which is shorter than its diff:
```python
import functools
import math

import jax
import jax.numpy as jnp
from jax import lax
from jax.experimental import pallas as pl
from jax.experimental.pallas import tpu as pltpu
from jax.sharding import PartitionSpec as P

HD = 128
PAGE = 16
NZ = 4
NEG = -1e30
C2 = math.log2(math.e) / math.sqrt(HD)
MESH = pl.DeviceIdType.MESH
F32 = jnp.float32
BF16 = jnp.bfloat16


def iota(shape, dim):
    return lax.broadcasted_iota(jnp.int32, shape, dim)


def kernel(
    groups,
    nx,
    q_hbm,
    nk_hbm,
    nv_hbm,
    k_hbm,
    v_hbm,
    owner_hbm,
    fill_hbm,
    slot_hbm,
    w_hbm,
    out_ref,
    q_ref,
    nk_ref,
    nv_ref,
    owner_ref,
    fill_ref,
    slot_ref,
    table_ref,
    other_ref,
    k_ref,
    v_ref,
    w_ref,
    bias_ref,
    score_ref,
    weight_ref,
    line_ref,
    sib_ref,
    qall_ref,
    qout_ref,
    qmov_ref,
    aout_ref,
    arecv_ref,
    mout_ref,
    mrecv_ref,
    sout_ref,
    srecv_ref,
    precv_ref,
    zacc_ref,
    zstat_ref,
    att_ref,
    load_sem,
    line_send,
    line_recv,
    new_send,
    new_recv,
    slot_send,
    slot_recv,
    sib_send,
    sib_recv,
    q_send,
    q_recv,
    qm_send,
    qm_recv,
    a_send,
    a_recv,
    s_send,
    s_recv,
    m_send,
    m_recv,
    p_send,
    p_recv,
    z_send,
    z_recv,
    y_send,
    y_recv,
    o_send,
    o_recv,
):
    np_ = nx * 2
    tokens = k_ref.shape[0]
    pages = owner_ref.shape[1]
    g = lax.axis_index("group")
    t = lax.axis_index("tp")
    x = lax.div(t, 8)
    z = lax.rem(lax.div(t, 2), NZ)
    c = lax.rem(t, 2)
    pp = x * 2 + c
    partner = lax.rem(g + groups // 2, groups)
    sibling = (g, x * 8 + z * 2 + (1 - c))

    def at(group, k, cc):
        xk = lax.rem(x + k, nx)
        return xk * 2 + cc, (group, xk * 8 + z * 2 + cc)

    far = [k for k in (2, 1, 3) if k < nx]
    plane = [(k, cc) for k in far for cc in range(2)] + [(0, 1 - c)]
    near = [(0, 1 - c)] + [(k, cc) for k in (1, 3, 2) if k < nx for cc in range(2)]
    whole = [(k, cc) for k in (0, 1, 3, 2) if k < nx for cc in range(2)]
    line = []
    for other in (3 * (1 - lax.div(z, 2)), lax.rem(2 + 3 * z, 5), 1 + lax.rem(z, 2)):
        line.append((other, (g, x * 8 + other * 2 + c)))

    def remote(src, dst, send, recv, device):
        return pltpu.make_async_remote_copy(
            src_ref=src,
            dst_ref=dst,
            send_sem=send,
            recv_sem=recv,
            device_id=device,
            device_id_type=MESH,
        )

    sent = []

    def send(*args):
        copy = remote(*args)
        copy.start()
        sent.append(copy)

    def arrive(dst, recv):
        remote(dst, dst, slot_send, recv, sibling).wait_recv()

    def fetch(src, dst, at):
        copy = pltpu.make_async_copy(src, dst, load_sem.at[at])
        copy.start()
        return copy

    barrier = pltpu.get_barrier_semaphore()
    greeted = [device for _, device in line]
    greeted.append(at(partner, 0, c)[1])
    greeted += [at(g, k, cc)[1] for k, cc in plane]
    for device in greeted:
        pl.semaphore_signal(barrier, inc=1, device_id=device, device_id_type=MESH)

    first = [fetch(q_hbm.at[0], q_ref, 3), fetch(slot_hbm, table_ref, 9)]
    small = [
        fetch(slot_hbm, slot_ref, 8),
        fetch(nk_hbm.at[0], nk_ref, 4),
        fetch(nv_hbm.at[0], nv_ref, 5),
        fetch(owner_hbm, owner_ref, 6),
        fetch(fill_hbm, fill_ref, 7),
    ]
    loads = [fetch(k_hbm, k_ref, 0), fetch(v_hbm, v_ref, 1), fetch(w_hbm, w_ref, 2)]
    for copy in first:
        copy.wait()

    order = (
        iota((16, 16), 1)
        == 2 * lax.rem(iota((16, 16), 0), 8) + lax.div(iota((16, 16), 0), 8)
    ).astype(BF16)

    def by_step(ref):
        rows = ref[...].reshape(16, ref.shape[2])
        return jnp.dot(order, rows, preferred_element_type=F32).astype(BF16)

    query = by_step(q_ref)
    line_ref[z, 0] = query[:, :HD]
    line_ref[z, 1] = query[:, HD:]

    pl.semaphore_wait(barrier, len(greeted))

    send(table_ref, other_ref, slot_send, slot_recv, at(partner, 0, c)[1])
    for i, (other, device) in enumerate(line):
        send(
            line_ref.at[z, 0:2], line_ref.at[z, 0:2], line_send.at[i], line_recv.at[z], device
        )

    for copy in small:
        copy.wait()
    place = (iota((32, HD), 1) == iota((32, HD), 0) + 32 * lax.rem(t, 4)).astype(BF16)
    line_ref[z, 2] = jnp.dot(by_step(nk_ref), place, preferred_element_type=F32).astype(BF16)
    line_ref[z, 3] = jnp.dot(by_step(nv_ref), place, preferred_element_type=F32).astype(BF16)
    owned = jnp.where(
        jnp.broadcast_to(owner_ref[...], (8, pages)) == iota((8, pages), 0),
        jnp.broadcast_to(fill_ref[...], (8, pages)),
        0,
    )
    spread = (lax.div(iota((pages, tokens), 1), PAGE) == iota((pages, tokens), 0)).astype(BF16)
    held = jnp.dot(owned.astype(F32).astype(BF16), spread, preferred_element_type=F32)
    within = lax.rem(iota((8, tokens), 1), PAGE).astype(F32)
    bias_ref[...] = jnp.where(within < held, 0.0, NEG)

    slots = [slot_ref[0, r] for r in range(8)]
    sub8 = iota((8, HD), 0)
    lane8 = lax.rem(iota((8, HD), 1), 8)
    moving = jnp.zeros((8, HD), jnp.int32)
    moving_lane = jnp.zeros((8, HD), jnp.int32)
    for r in range(8):
        goes = jnp.where(slots[r] < 8, 1, 0)
        moving = jnp.where(sub8 == r, goes, moving)
        moving_lane = jnp.where(lane8 == r, goes, moving_lane)

    def moving_rows(count):
        return jnp.concatenate([moving] * (count // 8), axis=0) == 1

    row = iota((16, HD), 1)
    same = lax.div(row, 8) == iota((16, HD), 0)
    take = (same & (jnp.concatenate([moving_lane, moving_lane], axis=0) == 1)).astype(BF16)

    arrive(other_ref, slot_recv)
    wanted = jnp.where(other_ref[...] < 8, other_ref[...], 0)
    wanted = jnp.max(wanted, axis=1, keepdims=True)
    mover = jnp.where(other_ref[...] < 8, iota((1, 8), 1), 0)
    mover = jnp.max(mover, axis=1, keepdims=True)
    lane16 = lax.rem(iota((2 * np_, HD), 1), 8)
    from_lane = lane16 == jnp.broadcast_to(mover, (2 * np_, HD))
    to_lane = lane16 == jnp.broadcast_to(wanted, (2 * np_, HD))
    fetch_row = (same & (lax.rem(row, 8) == jnp.broadcast_to(wanted, (16, HD)))).astype(BF16)
    for other, _ in line:
        arrive(line_ref.at[other, 0:2], line_recv.at[other])
    lines = [line_ref[i, e] for i in range(NZ) for e in range(2)]
    for i in range(NZ):
        for e in range(2):
            qall_ref[pp, i, e] = lines[2 * i + e]
    qout_ref[...] = jnp.dot(
        fetch_row, jnp.concatenate(lines, axis=0), preferred_element_type=F32
    ).astype(BF16)
    for i, (k, cc) in enumerate(whole):
        send(qout_ref, qmov_ref.at[pp], qm_send.at[i], qm_recv.at[pp], at(partner, k, cc)[1])
    for i, (k, cc) in enumerate(near):
        send(qall_ref.at[pp], qall_ref.at[pp], q_send.at[i], q_recv.at[pp], at(g, k, cc)[1])
    for i, (other, device) in enumerate(line):
        send(line_ref.at[z, 2:4], line_ref.at[z, 2:4], new_send.at[i], new_recv.at[z], device)

    lane = iota((HD, HD), 1)
    loads[0].wait()
    loads[1].wait()

    keep = jnp.where(moving_rows(16), 0.0, 1.0).astype(BF16)
    keep = jnp.concatenate([keep] * 8, axis=0)
    spread8 = (
        (iota((HD, 16), 1) == lax.div(iota((HD, 16), 0), 8)) & moving_rows(HD)[:, 0:16]
    ).astype(BF16)

    def head(k, b):
        return pl.ds(pl.multiple_of((lax.rem(x + k, nx) * 2 + b) * HD, HD), HD)

    def score(k, b):
        xk = lax.rem(x + k, nx)
        query = jnp.concatenate(
            [qall_ref[xk * 2 + cc, 2 * b : 2 * b + 2].reshape(64, HD) for cc in range(2)], axis=0
        )
        moved = jnp.concatenate(
            [qmov_ref[xk * 2 + cc].astype(F32)[8 * b : 8 * b + 8] for cc in range(2)], axis=0
        ).astype(BF16)
        moved = jnp.dot(spread8, moved, preferred_element_type=F32).astype(BF16)
        query = query * keep + moved
        score = lax.dot_general(
            query, k_ref[:, head(k, b)], (((1,), (1,)), ((), ())), preferred_element_type=F32
        )
        score = (score.reshape(16, 8, tokens) + bias_ref[...][None]).reshape(HD, tokens)
        score_ref[k % 2, b] = score
        return jnp.max(score, axis=1, keepdims=True)

    def weigh(k, b, top):
        weight = jnp.exp2((score_ref[k % 2, b] - top) * C2)
        weight_ref[k % 2, b] = weight.astype(BF16)
        return jnp.sum(weight, axis=1, keepdims=True)

    def gather(k, b):
        acc = jnp.dot(weight_ref[k % 2, b], v_ref[:, head(k, b)], preferred_element_type=F32)
        acc = acc.astype(BF16)
        for cc in range(2):
            aout_ref[k, cc, b] = acc[cc * 64 : cc * 64 + 64]
        return jnp.dot(take, acc, preferred_element_type=F32)

    def ready(k):
        for cc in range(2):
            source, _ = at(g, k, cc)
            arrive(qmov_ref.at[source], qm_recv.at[source])
        for cc in range(2) if k else (1 - c,):
            source, _ = at(g, k, cc)
            arrive(qall_ref.at[source], q_recv.at[source])

    def pass_on(k, tops, sums, few):
        stat = jnp.zeros((HD, HD), F32)
        for cc in range(2):
            part = slice(cc * 64, cc * 64 + 64)
            rows = slice(cc * 8, cc * 8 + 8)
            top = jnp.concatenate([tops[0][part], tops[1][part]], axis=0)
            total = jnp.concatenate([sums[0][part], sums[1][part]], axis=0)
            stat = jnp.where(lane == cc * 8, top, jnp.where(lane == cc * 8 + 1, total, stat))
            mout_ref[k, cc] = jnp.concatenate([few[0][rows], few[1][rows]], axis=0).astype(BF16)
        stat = stat.T
        for cc in range(2):
            sout_ref[k, cc] = stat[cc * 8 : cc * 8 + 8]
        for cc in range(2):
            i = k * 2 + cc
            device = at(partner, k, cc)[1]
            send(sout_ref.at[k, cc], precv_ref.at[pp], p_send.at[i], p_recv.at[pp], device)
            send(mout_ref.at[k, cc], mrecv_ref.at[pp], m_send.at[i], m_recv.at[pp], device)
        for cc in range(2) if k else (1 - c,):
            i = k * 2 + cc
            device = at(g, k, cc)[1]
            send(sout_ref.at[k, cc], srecv_ref.at[pp], s_send.at[i], s_recv.at[pp], device)
            send(aout_ref.at[k, cc], arecv_ref.at[pp], a_send.at[i], a_recv.at[pp], device)

    turns = [k for k in (1, 2, 3, 0) if k < nx]
    ready(turns[0])
    tops = [score(turns[0], b) for b in range(2)]
    for k, after in zip(turns, turns[1:] + [None]):
        if after is not None:
            ready(after)
        later, sums = [], []
        for b in range(2):
            if after is not None:
                later.append(score(after, b))
            sums.append(weigh(k, b, tops[b]))
        pass_on(k, tops, sums, [gather(k, b) for b in range(2)])
        tops = later
    for other, _ in line:
        arrive(line_ref.at[other, 2:4], new_recv.at[other])
    send(line_ref.at[:, 2:4], sib_ref, sib_send, sib_recv, sibling)
    arecv_ref[pp] = aout_ref[0, c]
    srecv_ref[pp] = sout_ref[0, c]

    arrive(sib_ref, sib_recv)
    tops, sums, news = [], [], []
    late = lax.rem(iota((8, 8, HD), 0), 2) == 1
    for b in range(2):
        new = [
            sum(
                line_ref[2 * b + i, 2 + kv].astype(F32) + sib_ref[2 * b + i, kv].astype(F32)
                for i in range(2)
            )
            for kv in range(2)
        ]
        query = line_ref[2 * b : 2 * b + 2, 0:2].astype(F32).reshape(8, 8, HD)
        first = jnp.sum(query * new[0][0:8][None], axis=2, keepdims=True)
        second = jnp.sum(query * new[0][8:16][None], axis=2, keepdims=True)
        first = jnp.broadcast_to(first, (8, 8, HD))
        second = jnp.where(late, jnp.broadcast_to(second, (8, 8, HD)), NEG)
        top = jnp.maximum(first, second)
        first = jnp.exp2((first - top) * C2)
        second = jnp.exp2((second - top) * C2)
        tops.append(top.reshape(64, HD))
        sums.append((first + second).reshape(64, HD))
        news.append((first * new[1][0:8][None] + second * new[1][8:16][None]).reshape(64, HD))
    new_acc = jnp.concatenate(news, axis=0)
    new_stat = jnp.where(
        lane == 0,
        jnp.concatenate(tops, axis=0),
        jnp.where(lane == 1, jnp.concatenate(sums, axis=0), 0.0),
    ).T
    new_top, new_sum = new_stat[0:1], new_stat[1:2]

    for k, cc in whole:
        source, _ = at(g, k, cc)
        arrive(precv_ref.at[source], p_recv.at[source])
    came = jnp.concatenate(
        [precv_ref[i, kind : kind + 1] for kind in range(2) for i in range(np_)], axis=0
    )
    came = jnp.where(from_lane, came, NEG)
    for step in (1, 2, 4):
        low = lax.rem(lax.div(lane16, step), 2) == 0
        came = jnp.maximum(
            came, jnp.where(low, pltpu.roll(came, HD - step, 1), pltpu.roll(came, step, 1))
        )
    came = jnp.where(to_lane, came, jnp.where(iota((2 * np_, HD), 0) < np_, NEG, 0.0))
    for k, cc in plane:
        source, _ = at(g, k, cc)
        arrive(srecv_ref.at[source], s_recv.at[source])
    tops = jnp.concatenate([srecv_ref[i, 0:1] for i in range(np_)], axis=0)
    tops = jnp.where(jnp.broadcast_to(moving_lane[0:1] == 1, (np_, HD)), NEG, tops)
    tops = jnp.concatenate([tops, came[:np_]], axis=0)
    sums = [srecv_ref[i, 1:2] for i in range(np_)]
    sums = jnp.concatenate(sums + [came[np_:]], axis=0)
    top8 = jnp.max(tops, axis=0, keepdims=True)
    scale = jnp.exp2((tops - top8) * C2)
    sum8 = jnp.sum(scale * sums, axis=0, keepdims=True)
    zstat_ref[z] = jnp.where(sub8 == 0, top8, jnp.where(sub8 == 1, sum8, 0.0))
    for i, (other, device) in enumerate(line):
        send(zstat_ref.at[z], zstat_ref.at[z], y_send.at[i], y_recv.at[z], device)
    scale = scale.T
    for k, cc in whole:
        source, _ = at(g, k, cc)
        arrive(mrecv_ref.at[source], m_recv.at[source])
    acc = jnp.zeros((16, 8, HD), F32)
    for i in range(np_):
        weight = scale[:, np_ + i : np_ + i + 1].reshape(16, 8, 1)
        acc += weight * mrecv_ref[i].astype(F32)[:, None, :]
    acc = acc.reshape(HD, HD)
    for k, cc in plane:
        source, _ = at(g, k, cc)
        arrive(arecv_ref.at[source], a_recv.at[source])
    for i in range(np_):
        acc += scale[:, i : i + 1] * arecv_ref[i].reshape(HD, HD).astype(F32)
    zacc_ref[z] = acc.astype(BF16)
    for i, (other, device) in enumerate(line):
        send(zacc_ref.at[z], zacc_ref.at[z], z_send.at[i], z_recv.at[z], device)

    for other, _ in line:
        arrive(zstat_ref.at[other], y_recv.at[other])
    tops = jnp.concatenate([zstat_ref[i, 0:1] for i in range(NZ)] + [new_top] * 4, axis=0)
    sums = jnp.concatenate([zstat_ref[i, 1:2] for i in range(NZ)] + [new_sum] * 4, axis=0)
    top = jnp.max(tops, axis=0, keepdims=True)
    scale = jnp.exp2((tops - top) * C2)
    scale = jnp.where((sub8 <= NZ), scale, 0.0)
    scale = (scale / jnp.sum(scale * sums, axis=0, keepdims=True)).T
    acc = scale[:, NZ : NZ + 1] * new_acc
    for other, _ in line:
        arrive(zacc_ref.at[other], z_recv.at[other])
    for i in range(NZ):
        acc += scale[:, i : i + 1] * zacc_ref[i].astype(F32)
    att_ref[pp] = acc.astype(BF16)
    for i, (k, cc) in enumerate(plane):
        send(att_ref.at[pp], att_ref.at[pp], o_send.at[i], o_recv.at[pp], at(g, k, cc)[1])

    loads[2].wait()
    result = jnp.zeros((16, out_ref.shape[1]), F32)
    for k, cc in [(0, c)] + near:
        source, _ = at(g, k, cc)
        if k or cc is not c:
            arrive(att_ref.at[source], o_recv.at[source])
        block = att_ref[source]
        for i in range(NZ):
            head = lax.div(source, 2) * 8 + i * 2 + lax.rem(source, 2)
            rows = pl.ds(pl.multiple_of(head * 256, 256), 256)
            both = jnp.concatenate(
                [block[i * 32 : i * 32 + 16], block[i * 32 + 16 : i * 32 + 32]], axis=1
            )
            result += jnp.dot(both, w_ref[rows, :], preferred_element_type=F32)
    out_ref[...] = result.astype(BF16)
    for copy in sent:
        copy.wait_send()


def solution(mesh):
    groups, tp = mesh.shape["group"], mesh.shape["tp"]
    nx = tp // 8

    def per_device(queries, new_keys, new_values, key_pages, value_pages, owner, fill, slots, weight):
        tokens = key_pages.shape[1] * PAGE
        width = key_pages.shape[3]
        features, columns = weight.shape
        vmem = pl.BlockSpec(memory_space=pltpu.VMEM)
        hbm = pl.BlockSpec(memory_space=pltpu.HBM)
        np_ = 2 * nx
        dma = pltpu.SemaphoreType.DMA
        out = pl.pallas_call(
            functools.partial(kernel, groups, nx),
            out_shape=jax.ShapeDtypeStruct((16, columns), BF16),
            in_specs=[hbm] * 9,
            out_specs=vmem,
            scratch_shapes=[
                pltpu.VMEM(queries.shape[1:], BF16),
                pltpu.VMEM(new_keys.shape[1:], BF16),
                pltpu.VMEM(new_values.shape[1:], BF16),
                pltpu.VMEM(owner.shape, jnp.int32),
                pltpu.VMEM(fill.shape, jnp.int32),
                pltpu.SMEM(slots.shape, jnp.int32),
                pltpu.VMEM(slots.shape, jnp.int32),
                pltpu.VMEM(slots.shape, jnp.int32),
                pltpu.VMEM((tokens, width), BF16),
                pltpu.VMEM((tokens, width), BF16),
                pltpu.VMEM((features, columns), BF16),
                pltpu.VMEM((8, tokens), F32),
                pltpu.VMEM((2, 2, HD, tokens), F32),
                pltpu.VMEM((2, 2, HD, tokens), BF16),
                pltpu.VMEM((NZ, 4, 16, HD), BF16),
                pltpu.VMEM((NZ, 2, 16, HD), BF16),
                pltpu.VMEM((np_, NZ, 2, 16, HD), BF16),
                pltpu.VMEM((16, HD), BF16),
                pltpu.VMEM((np_, 16, HD), BF16),
                pltpu.VMEM((nx, 2, 2, 64, HD), BF16),
                pltpu.VMEM((np_, 2, 64, HD), BF16),
                pltpu.VMEM((nx, 2, 16, HD), BF16),
                pltpu.VMEM((np_, 16, HD), BF16),
                pltpu.VMEM((nx, 2, 8, HD), F32),
                pltpu.VMEM((np_, 8, HD), F32),
                pltpu.VMEM((np_, 8, HD), F32),
                pltpu.VMEM((NZ, HD, HD), BF16),
                pltpu.VMEM((NZ, 8, HD), F32),
                pltpu.VMEM((np_, HD, HD), BF16),
                dma((10,)),
                dma((3,)),
                dma((NZ,)),
                dma((3,)),
                dma((NZ,)),
                dma,
                dma,
                dma,
                dma,
            ]
            + [dma((np_,))] * 12
            + [dma((3,)), dma((NZ,))] * 2
            + [dma((np_,))] * 2,
            compiler_params=pltpu.CompilerParams(
                collective_id=0, has_side_effects=True, vmem_limit_bytes=40 << 20
            ),
        )(
            *[
                pltpu.with_memory_space_constraint(a, pltpu.HBM)
                for a in (
                    queries,
                    new_keys,
                    new_values,
                    key_pages[0].reshape(tokens, width),
                    value_pages[0].reshape(tokens, width),
                    owner,
                    fill,
                    slots,
                    weight,
                )
            ]
        )
        return out.reshape(2, 8, columns).transpose(1, 0, 2)[None]

    placed = (
        P("group", None, None, "tp"),
        P("group", None, None, "tp"),
        P("group", None, None, "tp"),
        P("group", "tp", None, None),
        P("group", "tp", None, None),
        P("group", "tp"),
        P("group", "tp"),
        P("group", None),
        P(None, "tp"),
    )
    return jax.shard_map(
        per_device,
        mesh=mesh,
        in_specs=placed,
        out_specs=P("group", None, None, "tp"),
        check_vma=False,
    )
```

time: 40.1 us -> 37.1 us (0.925)
  Pallas kernels: 38.6 us -> 36.4 us
  local copies, waits for them, and re-layouts: 1.3 us -> 0.61 us
    pallas_call x1, Pallas kernels: 38.6 us -> 36.4 us  [per_device(): pl.pallas_call(functools.partial(kernel, groups, nx), out_shape=jax.Shape...]
    reshape x1, local copies, waits for them, and re-layouts: 1.3 us -> 0.61 us  [per_device(): return out.reshape(2, 8, columns).transpose(1, 0, 2)[None]]
where the time goes in v3:
time: 37.1 us; the launch traced here: 37 us
  Pallas kernels  36.4 us (98%)
  local copies, waits for them, and re-layouts  0.61 us (2%)
    pallas_call x1, Pallas kernels, per_device(): pl.pallas_call(functools.partial(kernel, groups, nx), out_shape=jax.Shape...  36.4 us

profile of v3, /device:TPU:1, one launch (start us, length us, event | category | flops | bytes accessed | tf_op | source)
XLA Modules:
  0.0 37.0 jit_solution(10475718738021441024)
XLA Ops:
  0.0 36.4 %shard_map.91 = bf16[16,256]{1,0:T(8,128)(2,1)S(1)} custom-call(bf16[1,8,2,256]{3,2,1,0:T(2,128)(2,1)} %q_hbm.1, bf16[1,8,2,32]{3,2,1,0:T(2,128)(2,1)} %nk_hbm.1, bf16[1,8,2,32]{3,2,1,0:T(2,128)(2,1)} %nv_hbm.1, bf16[1024,1024]{1,0:T(8,128)(2,1)} %bitcast.9, bf16[1024,1024]{1,0:T(8,128)(2,1)} %bitcast.10, s32[1,64]{1,0:T(1,128)} %owner_hbm.1, ...), custom_call_target="tpu_custom_call" | custom-call | tf_op jit(solution)/shard_map/pallas_call | solution.py:456
  36.4 0.6 %copy.12 = bf16[2,8,256]{2,0,1:T(2,128)(2,1)} copy(bf16[2,8,256]{2,1,0:T(8,128)(2,1)S(1)} %bitcast.8) | data formatting | bytes 16384 | tf_op jit(solution)/shard_map/reshape | solution.py:523

commit v4 on v3

--- a/solution.py
+++ b/solution.py
@@ -50,6 +50,7 @@
     score_ref,
     weight_ref,
     line_ref,
+    fresh_ref,
     sib_ref,
     qall_ref,
     qout_ref,
@@ -126,12 +127,11 @@
             device_id_type=MESH,
         )
 
-    sent = []
-
     def send(*args):
-        copy = remote(*args)
-        copy.start()
-        sent.append(copy)
+        remote(*args).start()
+
+    def left(ref, sem):
+        remote(ref, ref, sem, slot_recv, sibling).wait_send()
 
     def arrive(dst, recv):
         remote(dst, dst, slot_send, recv, sibling).wait_recv()
@@ -176,16 +176,16 @@
     pl.semaphore_wait(barrier, len(greeted))
 
     send(table_ref, other_ref, slot_send, slot_recv, at(partner, 0, c)[1])
-    for i, (other, device) in enumerate(line):
+    for _, device in line:
         send(
-            line_ref.at[z, 0:2], line_ref.at[z, 0:2], line_send.at[i], line_recv.at[z], device
+            line_ref.at[z], line_ref.at[z], line_send, line_recv, device
         )
 
     for copy in small:
         copy.wait()
     place = (iota((32, HD), 1) == iota((32, HD), 0) + 32 * lax.rem(t, 4)).astype(BF16)
-    line_ref[z, 2] = jnp.dot(by_step(nk_ref), place, preferred_element_type=F32).astype(BF16)
-    line_ref[z, 3] = jnp.dot(by_step(nv_ref), place, preferred_element_type=F32).astype(BF16)
+    fresh_ref[z, 0] = jnp.dot(by_step(nk_ref), place, preferred_element_type=F32).astype(BF16)
+    fresh_ref[z, 1] = jnp.dot(by_step(nv_ref), place, preferred_element_type=F32).astype(BF16)
     owned = jnp.where(
         jnp.broadcast_to(owner_ref[...], (8, pages)) == iota((8, pages), 0),
         jnp.broadcast_to(fill_ref[...], (8, pages)),
@@ -222,8 +222,7 @@
     from_lane = lane16 == jnp.broadcast_to(mover, (2 * np_, HD))
     to_lane = lane16 == jnp.broadcast_to(wanted, (2 * np_, HD))
     fetch_row = (same & (lax.rem(row, 8) == jnp.broadcast_to(wanted, (16, HD)))).astype(BF16)
-    for other, _ in line:
-        arrive(line_ref.at[other, 0:2], line_recv.at[other])
+    arrive(line_ref.at[0:3], line_recv)
     lines = [line_ref[i, e] for i in range(NZ) for e in range(2)]
     for i in range(NZ):
         for e in range(2):
@@ -231,12 +230,14 @@
     qout_ref[...] = jnp.dot(
         fetch_row, jnp.concatenate(lines, axis=0), preferred_element_type=F32
     ).astype(BF16)
-    for i, (k, cc) in enumerate(whole):
-        send(qout_ref, qmov_ref.at[pp], qm_send.at[i], qm_recv.at[pp], at(partner, k, cc)[1])
-    for i, (k, cc) in enumerate(near):
-        send(qall_ref.at[pp], qall_ref.at[pp], q_send.at[i], q_recv.at[pp], at(g, k, cc)[1])
-    for i, (other, device) in enumerate(line):
-        send(line_ref.at[z, 2:4], line_ref.at[z, 2:4], new_send.at[i], new_recv.at[z], device)
+    for k, cc in whole:
+        turn = (nx - k) % nx
+        send(qout_ref, qmov_ref.at[pp], qm_send, qm_recv.at[turn], at(partner, k, cc)[1])
+    for k, cc in near:
+        turn = (nx - k) % nx
+        send(qall_ref.at[pp], qall_ref.at[pp], q_send, q_recv.at[turn], at(g, k, cc)[1])
+    for _, device in line:
+        send(fresh_ref.at[z], fresh_ref.at[z], new_send, new_recv, device)
 
     lane = iota((HD, HD), 1)
     loads[0].wait()
@@ -280,13 +281,12 @@
             aout_ref[k, cc, b] = acc[cc * 64 : cc * 64 + 64]
         return jnp.dot(take, acc, preferred_element_type=F32)
 
+    def chip(ref, k, count=2):
+        return ref.at[pl.ds(lax.rem(x + k, nx) * 2, count)]
+
     def ready(k):
-        for cc in range(2):
-            source, _ = at(g, k, cc)
-            arrive(qmov_ref.at[source], qm_recv.at[source])
-        for cc in range(2) if k else (1 - c,):
-            source, _ = at(g, k, cc)
-            arrive(qall_ref.at[source], q_recv.at[source])
+        arrive(chip(qmov_ref, k), qm_recv.at[k])
+        arrive(chip(qall_ref, k, 2 if k else 1), q_recv.at[k])
 
     def pass_on(k, tops, sums, few):
         stat = jnp.zeros((HD, HD), F32)
@@ -301,15 +301,13 @@
         for cc in range(2):
             sout_ref[k, cc] = stat[cc * 8 : cc * 8 + 8]
         for cc in range(2):
-            i = k * 2 + cc
             device = at(partner, k, cc)[1]
-            send(sout_ref.at[k, cc], precv_ref.at[pp], p_send.at[i], p_recv.at[pp], device)
-            send(mout_ref.at[k, cc], mrecv_ref.at[pp], m_send.at[i], m_recv.at[pp], device)
+            send(sout_ref.at[k, cc], precv_ref.at[pp], p_send, p_recv, device)
+            send(mout_ref.at[k, cc], mrecv_ref.at[pp], m_send, m_recv, device)
         for cc in range(2) if k else (1 - c,):
-            i = k * 2 + cc
             device = at(g, k, cc)[1]
-            send(sout_ref.at[k, cc], srecv_ref.at[pp], s_send.at[i], s_recv.at[pp], device)
-            send(aout_ref.at[k, cc], arecv_ref.at[pp], a_send.at[i], a_recv.at[pp], device)
+            send(sout_ref.at[k, cc], srecv_ref.at[pp], s_send, s_recv, device)
+            send(aout_ref.at[k, cc], arecv_ref.at[pp], a_send, a_recv, device)
 
     turns = [k for k in (1, 2, 3, 0) if k < nx]
     ready(turns[0])
@@ -324,9 +322,8 @@
             sums.append(weigh(k, b, tops[b]))
         pass_on(k, tops, sums, [gather(k, b) for b in range(2)])
         tops = later
-    for other, _ in line:
-        arrive(line_ref.at[other, 2:4], new_recv.at[other])
-    send(line_ref.at[:, 2:4], sib_ref, sib_send, sib_recv, sibling)
+    arrive(fresh_ref.at[0:3], new_recv)
+    send(fresh_ref, sib_ref, sib_send, sib_recv, sibling)
     arecv_ref[pp] = aout_ref[0, c]
     srecv_ref[pp] = sout_ref[0, c]
 
@@ -336,12 +333,12 @@
     for b in range(2):
         new = [
             sum(
-                line_ref[2 * b + i, 2 + kv].astype(F32) + sib_ref[2 * b + i, kv].astype(F32)
+                fresh_ref[2 * b + i, kv].astype(F32) + sib_ref[2 * b + i, kv].astype(F32)
                 for i in range(2)
             )
             for kv in range(2)
         ]
-        query = line_ref[2 * b : 2 * b + 2, 0:2].astype(F32).reshape(8, 8, HD)
+        query = line_ref[2 * b : 2 * b + 2].astype(F32).reshape(8, 8, HD)
         first = jnp.sum(query * new[0][0:8][None], axis=2, keepdims=True)
         second = jnp.sum(query * new[0][8:16][None], axis=2, keepdims=True)
         first = jnp.broadcast_to(first, (8, 8, HD))
@@ -360,9 +357,7 @@
     ).T
     new_top, new_sum = new_stat[0:1], new_stat[1:2]
 
-    for k, cc in whole:
-        source, _ = at(g, k, cc)
-        arrive(precv_ref.at[source], p_recv.at[source])
+    arrive(precv_ref, p_recv)
     came = jnp.concatenate(
         [precv_ref[i, kind : kind + 1] for kind in range(2) for i in range(np_)], axis=0
     )
@@ -373,9 +368,7 @@
             came, jnp.where(low, pltpu.roll(came, HD - step, 1), pltpu.roll(came, step, 1))
         )
     came = jnp.where(to_lane, came, jnp.where(iota((2 * np_, HD), 0) < np_, NEG, 0.0))
-    for k, cc in plane:
-        source, _ = at(g, k, cc)
-        arrive(srecv_ref.at[source], s_recv.at[source])
+    arrive(srecv_ref.at[0 : np_ - 1], s_recv)
     tops = jnp.concatenate([srecv_ref[i, 0:1] for i in range(np_)], axis=0)
     tops = jnp.where(jnp.broadcast_to(moving_lane[0:1] == 1, (np_, HD)), NEG, tops)
     tops = jnp.concatenate([tops, came[:np_]], axis=0)
@@ -385,28 +378,23 @@
     scale = jnp.exp2((tops - top8) * C2)
     sum8 = jnp.sum(scale * sums, axis=0, keepdims=True)
     zstat_ref[z] = jnp.where(sub8 == 0, top8, jnp.where(sub8 == 1, sum8, 0.0))
-    for i, (other, device) in enumerate(line):
-        send(zstat_ref.at[z], zstat_ref.at[z], y_send.at[i], y_recv.at[z], device)
+    for _, device in line:
+        send(zstat_ref.at[z], zstat_ref.at[z], y_send, y_recv, device)
     scale = scale.T
-    for k, cc in whole:
-        source, _ = at(g, k, cc)
-        arrive(mrecv_ref.at[source], m_recv.at[source])
+    arrive(mrecv_ref, m_recv)
     acc = jnp.zeros((16, 8, HD), F32)
     for i in range(np_):
         weight = scale[:, np_ + i : np_ + i + 1].reshape(16, 8, 1)
         acc += weight * mrecv_ref[i].astype(F32)[:, None, :]
     acc = acc.reshape(HD, HD)
-    for k, cc in plane:
-        source, _ = at(g, k, cc)
-        arrive(arecv_ref.at[source], a_recv.at[source])
+    arrive(arecv_ref.at[0 : np_ - 1], a_recv)
     for i in range(np_):
         acc += scale[:, i : i + 1] * arecv_ref[i].reshape(HD, HD).astype(F32)
     zacc_ref[z] = acc.astype(BF16)
-    for i, (other, device) in enumerate(line):
-        send(zacc_ref.at[z], zacc_ref.at[z], z_send.at[i], z_recv.at[z], device)
-
-    for other, _ in line:
-        arrive(zstat_ref.at[other], y_recv.at[other])
+    for _, device in line:
+        send(zacc_ref.at[z], zacc_ref.at[z], z_send, z_recv, device)
+
+    arrive(zstat_ref.at[0:3], y_recv)
     tops = jnp.concatenate([zstat_ref[i, 0:1] for i in range(NZ)] + [new_top] * 4, axis=0)
     sums = jnp.concatenate([zstat_ref[i, 1:2] for i in range(NZ)] + [new_sum] * 4, axis=0)
     top = jnp.max(tops, axis=0, keepdims=True)
@@ -414,20 +402,22 @@
     scale = jnp.where((sub8 <= NZ), scale, 0.0)
     scale = (scale / jnp.sum(scale * sums, axis=0, keepdims=True)).T
     acc = scale[:, NZ : NZ + 1] * new_acc
-    for other, _ in line:
-        arrive(zacc_ref.at[other], z_recv.at[other])
+    arrive(zacc_ref.at[0:3], z_recv)
     for i in range(NZ):
         acc += scale[:, i : i + 1] * zacc_ref[i].astype(F32)
     att_ref[pp] = acc.astype(BF16)
-    for i, (k, cc) in enumerate(plane):
-        send(att_ref.at[pp], att_ref.at[pp], o_send.at[i], o_recv.at[pp], at(g, k, cc)[1])
+    for k, cc in plane:
+        turn = (nx - k) % nx
+        send(att_ref.at[pp], att_ref.at[pp], o_send, o_recv.at[turn], at(g, k, cc)[1])
 
     loads[2].wait()
     result = jnp.zeros((16, out_ref.shape[1]), F32)
     for k, cc in [(0, c)] + near:
         source, _ = at(g, k, cc)
-        if k or cc is not c:
-            arrive(att_ref.at[source], o_recv.at[source])
+        if k and cc == 0:
+            arrive(chip(att_ref, k), o_recv.at[k])
+        elif k == 0 and cc is not c:
+            arrive(att_ref.at[source], o_recv.at[k])
         block = att_ref[source]
         for i in range(NZ):
             head = lax.div(source, 2) * 8 + i * 2 + lax.rem(source, 2)
@@ -437,8 +427,19 @@
             )
             result += jnp.dot(both, w_ref[rows, :], preferred_element_type=F32)
     out_ref[...] = result.astype(BF16)
-    for copy in sent:
-        copy.wait_send()
+    left(table_ref, slot_send)
+    left(line_ref.at[0:3], line_send)
+    left(fresh_ref.at[0:3], new_send)
+    left(fresh_ref, sib_send)
+    left(qall_ref.at[0 : np_ - 1], q_send)
+    left(qmov_ref, qm_send)
+    left(arecv_ref.at[0 : np_ - 1], a_send)
+    left(srecv_ref.at[0 : np_ - 1], s_send)
+    left(mrecv_ref, m_send)
+    left(precv_ref, p_send)
+    left(zacc_ref.at[0:3], z_send)
+    left(zstat_ref.at[0:3], y_send)
+    left(att_ref.at[0 : np_ - 1], o_send)
 
 
 def solution(mesh):
@@ -473,7 +474,8 @@
                 pltpu.VMEM((8, tokens), F32),
                 pltpu.VMEM((2, 2, HD, tokens), F32),
                 pltpu.VMEM((2, 2, HD, tokens), BF16),
-                pltpu.VMEM((NZ, 4, 16, HD), BF16),
+                pltpu.VMEM((NZ, 2, 16, HD), BF16),
+                pltpu.VMEM((NZ, 2, 16, HD), BF16),
                 pltpu.VMEM((NZ, 2, 16, HD), BF16),
                 pltpu.VMEM((np_, NZ, 2, 16, HD), BF16),
                 pltpu.VMEM((16, HD), BF16),
@@ -489,18 +491,11 @@
                 pltpu.VMEM((NZ, 8, HD), F32),
                 pltpu.VMEM((np_, HD, HD), BF16),
                 dma((10,)),
-                dma((3,)),
-                dma((NZ,)),
-                dma((3,)),
-                dma((NZ,)),
-                dma,
-                dma,
-                dma,
-                dma,
             ]
-            + [dma((np_,))] * 12
-            + [dma((3,)), dma((NZ,))] * 2
-            + [dma((np_,))] * 2,
+            + [dma] * 8
+            + [dma, dma((nx,))] * 2
+            + [dma] * 12
+            + [dma, dma((nx,))],
             compiler_params=pltpu.CompilerParams(
                 collective_id=0, has_side_effects=True, vmem_limit_bytes=40 << 20
             ),

time: 37.1 us -> 36 us (0.970)
  Pallas kernels: 36.4 us -> 35.3 us
    pallas_call x1, Pallas kernels: 36.4 us -> 35.3 us  [per_device(): pl.pallas_call(functools.partial(kernel, groups, nx), out_shape=jax.Shape...]
where the time goes in v4:
time: 36 us; the launch traced here: 35.9 us
  Pallas kernels  35.3 us (98%)
  local copies, waits for them, and re-layouts  0.61 us (2%)
    pallas_call x1, Pallas kernels, per_device(): pl.pallas_call(functools.partial(kernel, groups, nx), out_shape=jax.Shape...  35.3 us

profile of v4, /device:TPU:1, one launch (start us, length us, event | category | flops | bytes accessed | tf_op | source)
XLA Modules:
  0.0 35.9 jit_solution(10691743976223839748)
XLA Ops:
  0.0 35.3 %shard_map.91 = bf16[16,256]{1,0:T(8,128)(2,1)S(1)} custom-call(bf16[1,8,2,256]{3,2,1,0:T(2,128)(2,1)} %q_hbm.1, bf16[1,8,2,32]{3,2,1,0:T(2,128)(2,1)} %nk_hbm.1, bf16[1,8,2,32]{3,2,1,0:T(2,128)(2,1)} %nv_hbm.1, bf16[1024,1024]{1,0:T(8,128)(2,1)} %bitcast.9, bf16[1024,1024]{1,0:T(8,128)(2,1)} %bitcast.10, s32[1,64]{1,0:T(1,128)} %owner_hbm.1, ...), custom_call_target="tpu_custom_call" | custom-call | tf_op jit(solution)/shard_map/pallas_call | solution.py:457
  35.3 0.6 %copy.12 = bf16[2,8,256]{2,0,1:T(2,128)(2,1)} copy(bf16[2,8,256]{2,1,0:T(8,128)(2,1)S(1)} %bitcast.8) | data formatting | bytes 16384 | tf_op jit(solution)/shard_map/reshape | solution.py:518

commit v5 on v4

--- a/solution.py
+++ b/solution.py
@@ -178,8 +178,22 @@
     send(table_ref, other_ref, slot_send, slot_recv, at(partner, 0, c)[1])
     for _, device in line:
         send(
-            line_ref.at[z], line_ref.at[z], line_send, line_recv, device
+            line_ref.at[z], line_ref.at[z], line_send, line_recv.at[z], device
         )
+
+    def relay(other):
+        qall_ref[pp, other] = line_ref[other]
+        for k, cc in near:
+            turn = (nx - k) % nx
+            send(
+                line_ref.at[other],
+                qall_ref.at[pp, other],
+                q_send,
+                q_recv.at[turn],
+                at(g, k, cc)[1],
+            )
+
+    relay(z)
 
     for copy in small:
         copy.wait()
@@ -213,6 +227,9 @@
     same = lax.div(row, 8) == iota((16, HD), 0)
     take = (same & (jnp.concatenate([moving_lane, moving_lane], axis=0) == 1)).astype(BF16)
 
+    for other, _ in line[:0:-1]:
+        arrive(line_ref.at[other], line_recv.at[other])
+        relay(other)
     arrive(other_ref, slot_recv)
     wanted = jnp.where(other_ref[...] < 8, other_ref[...], 0)
     wanted = jnp.max(wanted, axis=1, keepdims=True)
@@ -222,20 +239,16 @@
     from_lane = lane16 == jnp.broadcast_to(mover, (2 * np_, HD))
     to_lane = lane16 == jnp.broadcast_to(wanted, (2 * np_, HD))
     fetch_row = (same & (lax.rem(row, 8) == jnp.broadcast_to(wanted, (16, HD)))).astype(BF16)
-    arrive(line_ref.at[0:3], line_recv)
+    last = line[0][0]
+    arrive(line_ref.at[last], line_recv.at[last])
     lines = [line_ref[i, e] for i in range(NZ) for e in range(2)]
-    for i in range(NZ):
-        for e in range(2):
-            qall_ref[pp, i, e] = lines[2 * i + e]
     qout_ref[...] = jnp.dot(
         fetch_row, jnp.concatenate(lines, axis=0), preferred_element_type=F32
     ).astype(BF16)
     for k, cc in whole:
         turn = (nx - k) % nx
         send(qout_ref, qmov_ref.at[pp], qm_send, qm_recv.at[turn], at(partner, k, cc)[1])
-    for k, cc in near:
-        turn = (nx - k) % nx
-        send(qall_ref.at[pp], qall_ref.at[pp], q_send, q_recv.at[turn], at(g, k, cc)[1])
+    relay(last)
     for _, device in line:
         send(fresh_ref.at[z], fresh_ref.at[z], new_send, new_recv, device)
 
@@ -492,7 +505,8 @@
                 pltpu.VMEM((np_, HD, HD), BF16),
                 dma((10,)),
             ]
-            + [dma] * 8
+            + [dma, dma((NZ,))]
+            + [dma] * 6
             + [dma, dma((nx,))] * 2
             + [dma] * 12
             + [dma, dma((nx,))],

time: 36 us -> 35.9 us (level)
  no operation moved by 1% of the time
where the time goes in v5:
time: 35.9 us; the launch traced here: 35.7 us
  Pallas kernels  35.1 us (98%)
  local copies, waits for them, and re-layouts  0.61 us (2%)
    pallas_call x1, Pallas kernels, per_device(): pl.pallas_call(functools.partial(kernel, groups, nx), out_shape=jax.Shape...  35.1 us

profile of v5, /device:TPU:1, one launch (start us, length us, event | category | flops | bytes accessed | tf_op | source)
XLA Modules:
  0.0 35.7 jit_solution(13821776639202711483)
XLA Ops:
  0.0 35.1 %shard_map.91 = bf16[16,256]{1,0:T(8,128)(2,1)S(1)} custom-call(bf16[1,8,2,256]{3,2,1,0:T(2,128)(2,1)} %q_hbm.1, bf16[1,8,2,32]{3,2,1,0:T(2,128)(2,1)} %nk_hbm.1, bf16[1,8,2,32]{3,2,1,0:T(2,128)(2,1)} %nv_hbm.1, bf16[1024,1024]{1,0:T(8,128)(2,1)} %bitcast.9, bf16[1024,1024]{1,0:T(8,128)(2,1)} %bitcast.10, s32[1,64]{1,0:T(1,128)} %owner_hbm.1, ...), custom_call_target="tpu_custom_call" | custom-call | tf_op jit(solution)/shard_map/pallas_call | solution.py:470
  35.1 0.6 %copy.12 = bf16[2,8,256]{2,0,1:T(2,128)(2,1)} copy(bf16[2,8,256]{2,1,0:T(8,128)(2,1)S(1)} %bitcast.8) | data formatting | bytes 16384 | tf_op jit(solution)/shard_map/reshape | solution.py:532

commit v6 on v4

--- a/solution.py
+++ b/solution.py
@@ -66,31 +66,20 @@
     zstat_ref,
     att_ref,
     load_sem,
-    line_send,
+    all_send,
     line_recv,
-    new_send,
     new_recv,
     slot_send,
     slot_recv,
-    sib_send,
     sib_recv,
-    q_send,
     q_recv,
-    qm_send,
     qm_recv,
-    a_send,
     a_recv,
-    s_send,
     s_recv,
-    m_send,
     m_recv,
-    p_send,
     p_recv,
-    z_send,
     z_recv,
-    y_send,
     y_recv,
-    o_send,
     o_recv,
 ):
     np_ = nx * 2
@@ -178,7 +167,7 @@
     send(table_ref, other_ref, slot_send, slot_recv, at(partner, 0, c)[1])
     for _, device in line:
         send(
-            line_ref.at[z], line_ref.at[z], line_send, line_recv, device
+            line_ref.at[z], line_ref.at[z], all_send, line_recv, device
         )
 
     for copy in small:
@@ -232,12 +221,12 @@
     ).astype(BF16)
     for k, cc in whole:
         turn = (nx - k) % nx
-        send(qout_ref, qmov_ref.at[pp], qm_send, qm_recv.at[turn], at(partner, k, cc)[1])
+        send(qout_ref, qmov_ref.at[pp], all_send, qm_recv.at[turn], at(partner, k, cc)[1])
     for k, cc in near:
         turn = (nx - k) % nx
-        send(qall_ref.at[pp], qall_ref.at[pp], q_send, q_recv.at[turn], at(g, k, cc)[1])
+        send(qall_ref.at[pp], qall_ref.at[pp], all_send, q_recv.at[turn], at(g, k, cc)[1])
     for _, device in line:
-        send(fresh_ref.at[z], fresh_ref.at[z], new_send, new_recv, device)
+        send(fresh_ref.at[z], fresh_ref.at[z], all_send, new_recv, device)
 
     lane = iota((HD, HD), 1)
     loads[0].wait()
@@ -302,12 +291,12 @@
             sout_ref[k, cc] = stat[cc * 8 : cc * 8 + 8]
         for cc in range(2):
             device = at(partner, k, cc)[1]
-            send(sout_ref.at[k, cc], precv_ref.at[pp], p_send, p_recv, device)
-            send(mout_ref.at[k, cc], mrecv_ref.at[pp], m_send, m_recv, device)
+            send(sout_ref.at[k, cc], precv_ref.at[pp], all_send, p_recv, device)
+            send(mout_ref.at[k, cc], mrecv_ref.at[pp], all_send, m_recv, device)
         for cc in range(2) if k else (1 - c,):
             device = at(g, k, cc)[1]
-            send(sout_ref.at[k, cc], srecv_ref.at[pp], s_send, s_recv, device)
-            send(aout_ref.at[k, cc], arecv_ref.at[pp], a_send, a_recv, device)
+            send(sout_ref.at[k, cc], srecv_ref.at[pp], all_send, s_recv, device)
+            send(aout_ref.at[k, cc], arecv_ref.at[pp], all_send, a_recv, device)
 
     turns = [k for k in (1, 2, 3, 0) if k < nx]
     ready(turns[0])
@@ -323,7 +312,7 @@
         pass_on(k, tops, sums, [gather(k, b) for b in range(2)])
         tops = later
     arrive(fresh_ref.at[0:3], new_recv)
-    send(fresh_ref, sib_ref, sib_send, sib_recv, sibling)
+    send(fresh_ref, sib_ref, all_send, sib_recv, sibling)
     arecv_ref[pp] = aout_ref[0, c]
     srecv_ref[pp] = sout_ref[0, c]
 
@@ -379,7 +368,7 @@
     sum8 = jnp.sum(scale * sums, axis=0, keepdims=True)
     zstat_ref[z] = jnp.where(sub8 == 0, top8, jnp.where(sub8 == 1, sum8, 0.0))
     for _, device in line:
-        send(zstat_ref.at[z], zstat_ref.at[z], y_send, y_recv, device)
+        send(zstat_ref.at[z], zstat_ref.at[z], all_send, y_recv, device)
     scale = scale.T
     arrive(mrecv_ref, m_recv)
     acc = jnp.zeros((16, 8, HD), F32)
@@ -392,7 +381,7 @@
         acc += scale[:, i : i + 1] * arecv_ref[i].reshape(HD, HD).astype(F32)
     zacc_ref[z] = acc.astype(BF16)
     for _, device in line:
-        send(zacc_ref.at[z], zacc_ref.at[z], z_send, z_recv, device)
+        send(zacc_ref.at[z], zacc_ref.at[z], all_send, z_recv, device)
 
     arrive(zstat_ref.at[0:3], y_recv)
     tops = jnp.concatenate([zstat_ref[i, 0:1] for i in range(NZ)] + [new_top] * 4, axis=0)
@@ -408,7 +397,7 @@
     att_ref[pp] = acc.astype(BF16)
     for k, cc in plane:
         turn = (nx - k) % nx
-        send(att_ref.at[pp], att_ref.at[pp], o_send, o_recv.at[turn], at(g, k, cc)[1])
+        send(att_ref.at[pp], att_ref.at[pp], all_send, o_recv.at[turn], at(g, k, cc)[1])
 
     loads[2].wait()
     result = jnp.zeros((16, out_ref.shape[1]), F32)
@@ -428,18 +417,8 @@
             result += jnp.dot(both, w_ref[rows, :], preferred_element_type=F32)
     out_ref[...] = result.astype(BF16)
     left(table_ref, slot_send)
-    left(line_ref.at[0:3], line_send)
-    left(fresh_ref.at[0:3], new_send)
-    left(fresh_ref, sib_send)
-    left(qall_ref.at[0 : np_ - 1], q_send)
-    left(qmov_ref, qm_send)
-    left(arecv_ref.at[0 : np_ - 1], a_send)
-    left(srecv_ref.at[0 : np_ - 1], s_send)
-    left(mrecv_ref, m_send)
-    left(precv_ref, p_send)
-    left(zacc_ref.at[0:3], z_send)
-    left(zstat_ref.at[0:3], y_send)
-    left(att_ref.at[0 : np_ - 1], o_send)
+    blocks = 8 * (3 * (np_ - 1) + 3 + 1) + 2 * 6 + 3 * np_ + (np_ - 1) + 3
+    left(w_ref.at[0 : blocks * 16 * HD // w_ref.shape[1]], all_send)
 
 
 def solution(mesh):
@@ -492,10 +471,10 @@
                 pltpu.VMEM((np_, HD, HD), BF16),
                 dma((10,)),
             ]
-            + [dma] * 8
-            + [dma, dma((nx,))] * 2
-            + [dma] * 12
-            + [dma, dma((nx,))],
+            + [dma] * 6
+            + [dma((nx,))] * 2
+            + [dma] * 6
+            + [dma((nx,))],
             compiler_params=pltpu.CompilerParams(
                 collective_id=0, has_side_effects=True, vmem_limit_bytes=40 << 20
             ),

time: 36 us -> 35.9 us (level)
  no operation moved by 1% of the time
where the time goes in v6:
time: 35.9 us; the launch traced here: 35.8 us
  Pallas kernels  35.2 us (98%)
  local copies, waits for them, and re-layouts  0.61 us (2%)
    pallas_call x1, Pallas kernels, per_device(): pl.pallas_call(functools.partial(kernel, groups, nx), out_shape=jax.Shape...  35.2 us

profile of v6, /device:TPU:1, one launch (start us, length us, event | category | flops | bytes accessed | tf_op | source)
XLA Modules:
  0.0 35.8 jit_solution(11772973928087309172)
XLA Ops:
  0.0 35.2 %shard_map.91 = bf16[16,256]{1,0:T(8,128)(2,1)S(1)} custom-call(bf16[1,8,2,256]{3,2,1,0:T(2,128)(2,1)} %q_hbm.1, bf16[1,8,2,32]{3,2,1,0:T(2,128)(2,1)} %nk_hbm.1, bf16[1,8,2,32]{3,2,1,0:T(2,128)(2,1)} %nv_hbm.1, bf16[1024,1024]{1,0:T(8,128)(2,1)} %bitcast.9, bf16[1024,1024]{1,0:T(8,128)(2,1)} %bitcast.10, s32[1,64]{1,0:T(1,128)} %owner_hbm.1, ...), custom_call_target="tpu_custom_call" | custom-call | tf_op jit(solution)/shard_map/pallas_call | solution.py:436
  35.2 0.6 %copy.12 = bf16[2,8,256]{2,0,1:T(2,128)(2,1)} copy(bf16[2,8,256]{2,1,0:T(8,128)(2,1)S(1)} %bitcast.8) | data formatting | bytes 16384 | tf_op jit(solution)/shard_map/reshape | solution.py:497
